TPU v7x, 32 devices: a whole 2x2x4 slice. The times are simulated.
32 devices in a mesh: seq: 2 (over core), batch: 16 (over z, y, x).
Axes of the slice: x: 2, y: 2, z: 4, core: 2. Of those that a mesh axis runs over, the one named last changes fastest.
Arguments:
- tokens: bfloat16 [32, 1024, 768], P('batch', 'seq'), may hold values from -6 to 6
- grad_out: bfloat16 [32, 1024, 768], P('batch', 'seq'), may hold values from -6 to 6
- lengths: int32 [32], P('batch'), may hold values from 64 to 1024, as said below
- owners: int32 [288], replicated, may hold values from 0 to 31, as said below
- weight_slots: float32 [320, 32, 768], P(('seq', 'batch')), may hold values from -1 to 1
- first_slots: float32 [320, 32, 768], P(('seq', 'batch')), may hold values from -48.223551 to 48.223551
- second_slots: float32 [320, 32, 768], P(('seq', 'batch')), may hold values from 0.16384 to 94.37184
- small_params: float32 [12, 768], replicated, may hold values from -0.4 to 1.4
- small_first: float32 [12, 768], replicated, may hold values from -96 to 96
- small_second: float32 [12, 768], replicated, may hold values from 9.8304 to 163.84
- step_count: int32 [1], replicated, may hold values from 2 to 7
Outputs:
- layer_out: bfloat16 [32, 1024, 768], P('batch', 'seq')
- grad_in: float32 [32, 1024, 768], P('batch', 'seq')
- grad_slots: float32 [320, 32, 768], P(('seq', 'batch'))
- new_slots: float32 [320, 32, 768], P(('seq', 'batch'))
- new_first_slots: float32 [320, 32, 768], P(('seq', 'batch'))
- new_second_slots: float32 [320, 32, 768], P(('seq', 'batch'))
- small_grad: float32 [12, 768], replicated
- new_small: float32 [12, 768], replicated
- new_small_first: float32 [12, 768], replicated
- new_small_second: float32 [12, 768], replicated
Inputs may be any that keep to these rules, and one draw needn't show every extreme that they name: `lengths`: positions at or after a sequence's length are padding; some sequence has exactly 1024 live tokens and some exactly 64. `owners`: devices are numbered over seq and batch together, seq slowest. No device owns more than 10 panels, and some device owns exactly 10.
All inputs are finite; a program needn't handle non-finite values.
Results may differ from a plain program's by a relative error of at most 0.012.
Values may be sent and summed in bfloat16 or wider, within the bound.
No kernel may reach another device: no remote copies, remote signals or barrier semaphores. Data moves between devices by JAX's collectives and lax.ppermute only.
A program may use at most 192 MiB of HBM per device.

v0:
```python
from functools import partial
import math

import jax
import jax.numpy as jnp
from jax import lax
from jax.sharding import PartitionSpec as P

HEAD_DIM = 64


norm_eps = 1e-06
masked_score = -30.0
beta_first = 0.9
beta_second = 0.999
adam_eps = 1e-08
learn_rate = 0.2
decay_rate = 0.01


def slot_table(owners, capacity):
    panel_index = jnp.arange(owners.shape[0], dtype=jnp.int32)
    same_owner = (owners[:, None] == owners[None, :]) & (
        panel_index[None, :] < panel_index[:, None]
    )
    rank_within = jnp.sum(same_owner.astype(jnp.int32), axis=1)
    return owners * capacity + rank_within


def layer_norm(values, gain_row, shift_row):
    centre = values - jnp.mean(values, axis=-1, keepdims=True)
    spread = jnp.mean(centre * centre, axis=-1, keepdims=True)
    return centre * lax.rsqrt(spread + norm_eps) * gain_row + shift_row


def adam_update(weight, first_old, second_old, grad_now, step_count):
    step_float = step_count[0].astype(jnp.float32)
    first_new = beta_first * first_old + (1.0 - beta_first) * grad_now
    second_new = beta_second * second_old + (1.0 - beta_second) * grad_now * grad_now
    first_hat = first_new / (1.0 - jnp.power(beta_first, step_float))
    second_hat = second_new / (1.0 - jnp.power(beta_second, step_float))
    weight_new = weight - learn_rate * (
        first_hat / (jnp.sqrt(second_hat) + adam_eps) + decay_rate * weight
    )
    return (weight_new, first_new, second_new)


def product(left, right):
    return jnp.dot(left, right, preferred_element_type=jnp.float32)


def contract_rows(left, right):
    return lax.dot_general(
        left, right, (((0,), (0,)), ((), ())), preferred_element_type=jnp.float32
    )


def contract_cols(left, right):
    return lax.dot_general(
        left, right, (((1,), (1,)), ((), ())), preferred_element_type=jnp.float32
    )


def column_sum(matrix):
    return jnp.sum(matrix, axis=0, dtype=jnp.float32)


def local(
    tokens,
    grad_out,
    lengths,
    owners,
    weight_slots,
    first_slots,
    second_slots,
    small_params,
    small_first,
    small_second,
    step_count,
):
    capacity = weight_slots.shape[0]
    seq_count, block_rows, features = tokens.shape
    head_count = features // HEAD_DIM
    scale_factor = 1.0 / math.sqrt(HEAD_DIM)
    hidden_width = (small_params.shape[0] - 8) * features
    slot_of = slot_table(owners, capacity)
    sending = weight_slots.astype(jnp.bfloat16)
    gathered = lax.all_gather(sending, ("seq", "batch"), axis=0, tiled=True)
    weight_stack = jnp.take(gathered, slot_of, axis=0).reshape(-1, features)
    w_query = weight_stack[0:features]
    w_key = weight_stack[features : 2 * features]
    w_value = weight_stack[2 * features : 3 * features]
    w_out = weight_stack[3 * features : 4 * features]
    w_hidden = weight_stack[4 * features : 4 * features + hidden_width]
    w_down = weight_stack[4 * features + hidden_width :]
    gain_one = small_params[0]
    shift_one = small_params[1]
    gain_two = small_params[2]
    shift_two = small_params[3]
    bias_hidden = small_params[8:].reshape(-1)
    flat_tokens = tokens.reshape(-1, features)
    tokens_wide = flat_tokens.astype(jnp.float32)
    queries = (product(flat_tokens, w_query) + small_params[4]).astype(jnp.bfloat16)
    keys_low = product(flat_tokens, w_key).astype(jnp.bfloat16)
    values = (product(flat_tokens, w_value) + small_params[5]).astype(jnp.bfloat16)
    positions = lax.axis_index("seq") * block_rows + jnp.arange(block_rows, dtype=jnp.int32)
    live_keys = positions[None, :] < lengths[:, None]

    def split_heads(matrix):
        return matrix.reshape(seq_count, block_rows, head_count, HEAD_DIM)

    def block_scores(query_heads, key_heads, live_row):
        scores = (
            jnp.einsum("qhd,khd->hqk", query_heads, key_heads, preferred_element_type=jnp.float32)
            * scale_factor
        )
        return jnp.where(live_row[None, None, :], scores, masked_score)

    def attend(block_items):
        query_heads, key_heads, value_heads, live_row = block_items
        scores = block_scores(query_heads, key_heads, live_row)
        row_top = jnp.max(scores, axis=-1, keepdims=True)
        exp_scores = jnp.exp(scores - row_top)
        exp_total = jnp.sum(exp_scores, axis=-1, keepdims=True)
        probs_low = (exp_scores / exp_total).astype(jnp.bfloat16)
        context = jnp.einsum(
            "hqk,khd->qhd", probs_low, value_heads, preferred_element_type=jnp.float32
        )
        return (
            context.reshape(block_rows, features).astype(jnp.bfloat16),
            (row_top + jnp.log(exp_total))[..., 0],
        )

    context, log_total = lax.map(
        attend, (split_heads(queries), split_heads(keys_low), split_heads(values), live_keys)
    )
    context_flat = context.reshape(-1, features)
    attn_out = product(context_flat, w_out) + small_params[6]
    mixed_rows, norm_one_pull = jax.vjp(layer_norm, tokens_wide + attn_out, gain_one, shift_one)
    mixed_low = mixed_rows.astype(jnp.bfloat16).reshape(tokens.shape)
    ffn_in, cot_in = (
        lax.all_to_all(mixed_low, "seq", split_axis=0, concat_axis=1, tiled=True),
        lax.all_to_all(grad_out, "seq", split_axis=0, concat_axis=1, tiled=True),
    )
    ffn_rows = ffn_in.reshape(-1, features)
    cot_rows = cot_in.reshape(-1, features).astype(jnp.float32)
    hidden_pre = contract_cols(ffn_rows, w_hidden) + bias_hidden
    hidden_act, gelu_pull = jax.vjp(partial(jax.nn.gelu, approximate=False), hidden_pre)
    hidden_low = hidden_act.astype(jnp.bfloat16)
    residual = ffn_rows.astype(jnp.float32) + product(hidden_low, w_down) + small_params[7]
    layer_rows, norm_two_pull = jax.vjp(layer_norm, residual, gain_two, shift_two)
    d_residual, d_gain_two, d_shift_two = norm_two_pull(cot_rows)
    d_down = d_residual.astype(jnp.bfloat16)
    d_w_down = contract_rows(hidden_low, d_down)
    d_pre = gelu_pull(contract_cols(d_down, w_down))[0].astype(jnp.bfloat16)
    d_w_hidden = contract_rows(d_pre, ffn_rows)
    d_ffn_in = (d_residual + product(d_pre, w_hidden)).astype(jnp.bfloat16).reshape(ffn_in.shape)
    layer_low = layer_rows.astype(jnp.bfloat16).reshape(ffn_in.shape)
    layer_out, d_mixed = (
        lax.all_to_all(layer_low, "seq", split_axis=1, concat_axis=0, tiled=True),
        lax.all_to_all(d_ffn_in, "seq", split_axis=1, concat_axis=0, tiled=True),
    )
    d_summed, d_gain_one, d_shift_one = norm_one_pull(
        d_mixed.reshape(-1, features).astype(jnp.float32)
    )
    d_attn = d_summed.astype(jnp.bfloat16)
    d_w_out = contract_rows(context_flat, d_attn)
    d_context = contract_cols(d_attn, w_out).astype(jnp.bfloat16)

    def attend_back(block_items):
        query_heads, key_heads, value_heads, live_row, total_row, d_context_row = block_items
        scores = block_scores(query_heads, key_heads, live_row)
        probs = jnp.exp(scores - total_row[..., None])
        d_heads = d_context_row.reshape(block_rows, head_count, HEAD_DIM)
        d_probs = jnp.einsum(
            "qhd,khd->hqk", d_heads, value_heads, preferred_element_type=jnp.float32
        )
        row_delta = jnp.sum(probs * d_probs, axis=-1, keepdims=True)
        d_scores = jnp.where(live_row[None, None, :], probs * (d_probs - row_delta), 0.0).astype(
            jnp.bfloat16
        )
        d_query = (
            jnp.einsum("hqk,khd->qhd", d_scores, key_heads, preferred_element_type=jnp.float32)
            * scale_factor
        )
        d_key = (
            jnp.einsum("hqk,qhd->khd", d_scores, query_heads, preferred_element_type=jnp.float32)
            * scale_factor
        )
        d_value = jnp.einsum(
            "hqk,qhd->khd", probs.astype(jnp.bfloat16), d_heads, preferred_element_type=jnp.float32
        )
        query_out = d_query.reshape(block_rows, features).astype(jnp.bfloat16)
        key_out = d_key.reshape(block_rows, features).astype(jnp.bfloat16)
        value_out = d_value.reshape(block_rows, features).astype(jnp.bfloat16)
        return (query_out, key_out, value_out)

    d_query, d_key, d_value = lax.map(
        attend_back,
        (
            split_heads(queries),
            split_heads(keys_low),
            split_heads(values),
            live_keys,
            log_total,
            d_context.reshape(tokens.shape),
        ),
    )
    d_query = d_query.reshape(-1, features)
    d_key = d_key.reshape(-1, features)
    d_value = d_value.reshape(-1, features)
    grad_in = (
        d_summed
        + contract_cols(d_query, w_query)
        + contract_cols(d_key, w_key)
        + contract_cols(d_value, w_value)
    )
    grad_stack = jnp.concatenate(
        [
            contract_rows(flat_tokens, d_query),
            contract_rows(flat_tokens, d_key),
            contract_rows(flat_tokens, d_value),
            d_w_out,
            d_w_hidden,
            d_w_down,
        ],
        axis=0,
    )
    panels = grad_stack.reshape(-1, weight_slots.shape[1], features)
    devices = lax.axis_size("seq") * lax.axis_size("batch")
    slot_grads = (
        jnp.zeros((devices * capacity,) + weight_slots.shape[1:], jnp.float32)
        .at[slot_of]
        .set(panels)
    )
    grad_slots = lax.psum_scatter(slot_grads, ("seq", "batch"), scatter_dimension=0, tiled=True)
    small_rows = jnp.stack(
        [
            d_gain_one,
            d_shift_one,
            d_gain_two,
            d_shift_two,
            column_sum(d_query),
            column_sum(d_value),
            column_sum(d_attn),
            column_sum(d_down),
        ]
    )
    small_local = jnp.concatenate([small_rows, column_sum(d_pre).reshape(-1, features)], axis=0)
    small_grad = lax.psum(small_local, ("seq", "batch"))
    new_slots, new_first_slots, new_second_slots = adam_update(
        weight_slots, first_slots, second_slots, grad_slots, step_count
    )
    new_small, new_small_first, new_small_second = adam_update(
        small_params, small_first, small_second, small_grad, step_count
    )
    return (
        layer_out,
        grad_in.reshape(tokens.shape),
        grad_slots,
        new_slots,
        new_first_slots,
        new_second_slots,
        small_grad,
        new_small,
        new_small_first,
        new_small_second,
    )


def solution(mesh):
    in_specs = (
        P("batch", "seq", None),
        P("batch", "seq", None),
        P("batch"),
        P(),
        P(("seq", "batch"), None, None),
        P(("seq", "batch"), None, None),
        P(("seq", "batch"), None, None),
        P(),
        P(),
        P(),
        P(),
    )
    out_specs = (
        P("batch", "seq", None),
        P("batch", "seq", None),
        P(("seq", "batch"), None, None),
        P(("seq", "batch"), None, None),
        P(("seq", "batch"), None, None),
        P(("seq", "batch"), None, None),
        P(),
        P(),
        P(),
        P(),
    )
    return jax.shard_map(local, mesh=mesh, in_specs=in_specs, out_specs=out_specs, check_vma=False)
```

profile of v0, /device:TPU:0, one launch (start us, length us, event | category | flops | bytes accessed | tf_op | source)
XLA Modules:
  0.0 867.5 jit_solution(4834389363362749177)
XLA Ops:
  18.7 105.7 %all-gather.2.cloned.1.call-done = bf16[320,32,768]{2,1,0:T(8,128)(2,1)} async-done(((bf16[10,32,768]{2,1,0:T(8,128)(2,1)}), bf16[320,32,768]{2,1,0:T(8,128)(2,1)}) %all-gather.2.cloned.1.call-update) | async-done | bytes 15728656 | tf_op jit(solution)/shard_map/all_gather | solution.py:88
  124.3 17.6 %gather_fusion = bf16[288,32,768]{2,1,0:T(8,128)(2,1)} fusion(bf16[320,32,768]{2,1,0:T(8,128)(2,1)} %all-gather.2.cloned.1.call-done, s32[1024]{0:T(1024)S(1)} %pad_clamp_fusion), kind=kCustom, calls=%fused_computation | custom fusion | bytes 28312704 | tf_op jit(solution)/shard_map/jit(_take)/gather | solution.py:89
  142.0 7.8 broadcast_select_fusion
  156.5 8.8 %fusion.109 = (bf16[96,32,768]{2,1,0:T(8,128)(2,1)}, bf16[96,32,768]{2,1,0:T(8,128)(2,1)}) fusion(bf16[288,32,768]{2,1,0:T(8,128)(2,1)} %copy-done.2), kind=kLoop, calls=%fused_computation.173 | loop fusion | bytes 18874368 | tf_op jit(solution)/shard_map/slice | solution.py:95
  181.8 22.5 %while.26 = (s32[]{:T(128)}, bf16[2,512,768]{2,1,0:T(8,128)(2,1)}, f32[2,12,512]{2,1,0:T(8,128)S(1)}, bf16[2,512,12,64]{1,3,2,0:T(8,128)(2,1)}, pred[2,512]{1,0:...) while((s32[]{:T(128)}, bf16[2,512,768]{2,1,0:T(8,128)(2,1)}, ...), condition=%wide.region_4.5_spmd, body=%wide.region_1.4_spmd.sunk | while | flops 843442176 | bytes 50573436 | solution.py:134
  217.6 35.7 %multiply_convert_fusion.2 = (bf16[1024,3072]{1,0:T(8,128)(2,1)S(1)}, f32[1024,3072]{1,0:T(8,128)}, f32[1024,3072]{1,0:T(8,128)}) fusion(f32[3072]{0:T(1024)S(1)} %copy-done.69, bf16[1024,768]{1,0:T(8,128)(2,1)S(1)} %bitcast.198, bf16[3072,768]{1,0:T(8,128)(2,1)} %bitcast.204), kind=kOutput, calls=%fused_computation.81 | convolution fusion | flops 5039456256 | bytes 37761024 | tf_op jit(solution)/shard_map/dot_general | solution.py:59
  253.4 5.6 fusion.112
  266.2 18.1 %convert_reduce_fusion = (f32[3072]{0:T(1024)}, bf16[1024,3072]{1,0:T(8,128)(2,1)}) fusion(f32[1024,3072]{1,0:T(8,128)} %get-tuple-element.255, bf16[1024,768]{0,1:T(8,128)(2,1)S(1)} %get-tuple-element.242, bf16[3072,768]{1,0:T(8,128)(2,1)} %bitcast.206, f32[1024,3072]{1,0:T(8,128)} %get-tuple-element.271, f32[3072]{0:T(1024)S(1)} %copy-done.69), kind=kOutput, calls=%fused_computation.79 | convolution fusion | flops 4885312512 | bytes 37773312 | tf_op jit(solution)/shard_map/dot_general | solution.py:59
  284.3 9.5 %fusion.95 = bf16[1,1024,768]{1,2,0:T(8,128)(2,1)} fusion(bf16[1024,3072]{1,0:T(8,128)(2,1)} %get-tuple-element.275, bf16[3072,768]{1,0:T(8,128)(2,1)} %bitcast.205, f32[1024,768]{0,1:T(8,128)S(1)} %get-tuple-element.253, f32[1024]{0:T(1024)S(1)} %negate_multiply_fusion.2), kind=kOutput, calls=%fused_computation.132 | convolution fusion | flops 4834197504 | bytes 15732736 | tf_op jit(solution)/shard_map/dot_general | solution.py:49
  293.8 7.6 copy.127
  301.9 11.4 %reduce.28 = bf16[1024,768]{1,0:T(8,128)(2,1)} reduce(bf16[1024,1,768]{2,1,0:T(2,128)(2,1)S(1)} %bitcast.192, bf16[]{:T(256)} %broadcast.199), dimensions={1}, to_apply=%bitcast.106.reduce_sub_computation | reduce | bytes 3145730
  314.9 5.9 all_to_all.40
  333.1 138.2 %while.27 = (s32[]{:T(128)}, bf16[2,512,768]{1,2,0:T(8,128)(2,1)}, bf16[2,512,768]{1,2,0:T(8,128)(2,1)}, bf16[2,512,768]{1,2,0:T(8,128)(2,1)}, bf16[2,512,12,64]...) while((s32[]{:T(128)}, bf16[2,512,768]{1,2,0:T(8,128)(2,1)}, ...), condition=%wide.region_15.16_spmd, body=%wide.region_13.15_spmd.sunk | while | flops 2097034240 | bytes 179518224 | solution.py:198
  334.8 7.4 fusion.184
  342.2 7.4 fusion.185
  349.7 22.7 %multiply_convert_fusion.6 = bf16[12,64,512]{2,1,0:T(8,128)(2,1)S(1)} fusion(f32[12,512,512]{1,2,0:T(8,128)} %fusion.184, f32[12,512,512]{1,2,0:T(8,128)} %fusion.185, f32[12,512]{1,0:T(8,128)S(1)} %dynamic-slice_bitcast_fusion.2, pred[512]{0:T(512)(128)(4,1)S(1)} %dynamic-slice_reduce_fusion.5, ...), kind=kOutput, calls=%fused_computation.43.clone.1 | convolution fusion | flops 438049280 | bytes 51971584 | tf_op jit(solution)/shard_map/while/body/eval_jaxpr/hqk,qhd->khd/dot_general | solution.py:187
  372.5 7.7 fusion.186
  382.0 19.3 %multiply_convert_fusion.5 = bf16[12,64,512]{2,1,0:T(8,128)(2,1)S(1)} fusion(f32[12,512,512]{1,2,0:T(8,128)} %fusion.184, f32[12,512,512]{1,2,0:T(8,128)} %fusion.185, f32[12,512]{1,0:T(8,128)S(1)} %dynamic-slice_bitcast_fusion.2, pred[512]{0:T(512)(128)(4,1)S(1)} %dynamic-slice_reduce_fusion.5, bf16[2,512,12,64]{1,3,2,0:T(8,128)(2,1)} %get-tuple-element.440, ...), kind=kOutput, calls=%fused_computation.44.clone.1 | convolution fusion | flops 438049280 | bytes 51971584 | tf_op jit(solution)/shard_map/while/body/eval_jaxpr/hqk,khd->qhd/dot_general | solution.py:183
  403.7 7.4 fusion.184
  411.1 7.4 fusion.185
  418.6 22.7 %multiply_convert_fusion.6 = bf16[12,64,512]{2,1,0:T(8,128)(2,1)S(1)} fusion(f32[12,512,512]{1,2,0:T(8,128)} %fusion.184, f32[12,512,512]{1,2,0:T(8,128)} %fusion.185, f32[12,512]{1,0:T(8,128)S(1)} %dynamic-slice_bitcast_fusion.2, pred[512]{0:T(512)(128)(4,1)S(1)} %dynamic-slice_reduce_fusion.5, ...), kind=kOutput, calls=%fused_computation.43.clone.1 | convolution fusion | flops 438049280 | bytes 51971584 | tf_op jit(solution)/shard_map/while/body/eval_jaxpr/hqk,qhd->khd/dot_general | solution.py:187
  441.3 7.7 fusion.186
  450.8 19.2 %multiply_convert_fusion.5 = bf16[12,64,512]{2,1,0:T(8,128)(2,1)S(1)} fusion(f32[12,512,512]{1,2,0:T(8,128)} %fusion.184, f32[12,512,512]{1,2,0:T(8,128)} %fusion.185, f32[12,512]{1,0:T(8,128)S(1)} %dynamic-slice_bitcast_fusion.2, pred[512]{0:T(512)(128)(4,1)S(1)} %dynamic-slice_reduce_fusion.5, bf16[2,512,12,64]{1,3,2,0:T(8,128)(2,1)} %get-tuple-element.440, ...), kind=kOutput, calls=%fused_computation.44.clone.1 | convolution fusion | flops 438049280 | bytes 51971584 | tf_op jit(solution)/shard_map/while/body/eval_jaxpr/hqk,khd->qhd/dot_general | solution.py:183
  485.1 7.7 convolution_dynamic-update-slice_fusion.1
  492.7 7.6 convolution_dynamic-update-slice_fusion
  500.4 14.4 %broadcast_in_dim.93 = f32[320,32,768]{2,1,0:T(8,128)} broadcast(f32[]{:T(128)} %constant.81.clone.1), dimensions={} | broadcast | bytes 31457284 | tf_op jit(solution)/shard_map/broadcast_in_dim | solution.py:232
  514.8 61.8 %scatter_fusion = f32[320,32,768]{2,1,0:T(8,128)} fusion(f32[320,32,768]{2,1,0:T(8,128)} %broadcast_in_dim.93, s32[288]{0:T(512)S(1)} %copy-done.59, f32[288,32,768]{2,1,0:T(8,128)} %bitcast.45), kind=kCustom, calls=%fused_computation.1 | custom fusion | bytes 84935808 | tf_op jit(solution)/shard_map/scatter | solution.py:234
  585.6 7.5 copy.124
  593.1 11.4 %reduce.27 = bf16[1024,768]{1,0:T(8,128)(2,1)} reduce(bf16[1024,1,768]{2,1,0:T(2,128)(2,1)S(1)} %bitcast.193, bf16[]{:T(256)} %broadcast.199), dimensions={1}, to_apply=%bitcast.104.reduce_sub_computation | reduce | bytes 3145730
  606.3 6.5 all_to_all.41
  616.9 41.2 %psum.7 = f32[12,768]{1,0:T(8,128)S(1)} all-reduce(f32[12,768]{1,0:T(8,128)S(1)} %concatenate.7), channel_id=1, replica_groups=mesh['seq'=2,'batch'=16] {'seq','batch'}, use_global_device_ids=true, to_apply=%region_27.28 | all-reduce | flops 9216 | bytes 73728 | tf_op jit(solution)/shard_map/psum | solution.py:250
  668.2 189.0 %reduce-scatter.2.cloned.1.call-done = f32[10,32,768]{2,1,0:T(8,128)} async-done(((f32[320,32,768]{2,1,0:T(8,128)}), f32[10,32,768]{2,1,0:T(8,128)}) %reduce-scatter.2.cloned.1.call-update) | async-done | bytes 983056 | tf_op jit(solution)/shard_map/reduce_scatter | solution.py:236
  (288 shorter events, 140.9 us)
Async XLA Ops:
  7.2 6.0 slice-start
  7.2 117.1 %all-gather.2.cloned.1.call-start = ((), (), s32[]{:S(2)}) async-start(), calls=%async_computation.5 | async-start | bytes 16220160 | tf_op jit(solution)/shard_map/all_gather | solution.py:88
  9.3 6.2 all-to-all-start.2
  13.0 844.1 %reduce-scatter.2.cloned.1.call-start = ((), (), s32[]{:S(2)}) async-start(), calls=%async_computation.6 | async-start | bytes 32440320 | tf_op jit(solution)/shard_map/reduce_scatter | solution.py:236
  15.5 126.5 %copy-start.9 = (bf16[2,512,768]{2,1,0:T(8,128)(2,1)}, bf16[2,512,768]{2,1,0:T(8,128)(2,1)S(1)}, u32[]{:S(2)}) copy-start(bf16[2,512,768]{2,1,0:T(8,128)(2,1)S(1)} %all-to-all-done.2) | copy-start | bytes 4718596
  17.9 124.1 %copy-start.58 = (s32[288]{0:T(512)}, s32[288]{0:T(512)S(1)}, u32[]{:S(2)}) copy-start(s32[288]{0:T(512)S(1)} %get-tuple-element.257) | copy-start | bytes 3460
  156.5 8.8 %copy-start.19 = (bf16[24,32,768]{2,1,0:T(8,128)(2,1)}, bf16[24,32,768]{2,1,0:T(8,128)(2,1)S(1)}, u32[]{:S(2)}) copy-start(bf16[24,32,768]{2,1,0:T(8,128)(2,1)S(1)} %get-tuple-element.267) | copy-start | bytes 3538948
  156.5 8.8 %copy-start.73 = (bf16[2,512,768]{2,1,0:T(8,128)(2,1)S(1)}, bf16[2,512,768]{2,1,0:T(8,128)(2,1)}, u32[]{:S(2)}) copy-start(bf16[2,512,768]{2,1,0:T(8,128)(2,1)} %param.15) | copy-start | bytes 4718596
  181.8 22.5 %copy-start.71 = (f32[768]{0:T(1024)S(1)}, f32[768]{0:T(1024)}, u32[]{:S(2)}) copy-start(f32[768]{0:T(1024)} %get-tuple-element.200) | copy-start | bytes 9220
  209.3 6.7 copy-start.49
  210.4 7.2 copy-start.69
  215.9 37.4 %copy-start.16 = (bf16[2,512,768]{2,1,0:T(8,128)(2,1)}, bf16[2,512,768]{2,1,0:T(8,128)(2,1)S(1)}, u32[]{:S(2)}) copy-start(bf16[2,512,768]{2,1,0:T(8,128)(2,1)S(1)} %all_to_all.19) | copy-start | bytes 4718596
  217.6 35.7 %copy-start.21 = (bf16[96,32,768]{2,1,0:T(8,128)(2,1)S(1)}, bf16[96,32,768]{2,1,0:T(8,128)(2,1)}, u32[]{:S(2)}) copy-start(bf16[96,32,768]{2,1,0:T(8,128)(2,1)} %get-tuple-element.262) | copy-start | bytes 14155780
  217.6 35.7 %copy-start.27 = (bf16[1024,768]{0,1:T(8,128)(2,1)S(1)}, bf16[1024,768]{0,1:T(8,128)(2,1)}, u32[]{:S(2)}) copy-start(bf16[1024,768]{0,1:T(8,128)(2,1)} %copy.153) | copy-start | bytes 4718596
  217.6 35.7 %copy-start.70 = (f32[768]{0:T(1024)S(1)}, f32[768]{0:T(1024)}, u32[]{:S(2)}) copy-start(f32[768]{0:T(1024)} %get-tuple-element.197) | copy-start | bytes 9220
  266.2 18.1 %copy-start.28 = (bf16[1024,768]{0,1:T(8,128)(2,1)}, bf16[1024,768]{0,1:T(8,128)(2,1)S(1)}, u32[]{:S(2)}) copy-start(bf16[1024,768]{0,1:T(8,128)(2,1)S(1)} %get-tuple-element.242) | copy-start | bytes 4718596
  372.4 7.7 copy-start.12
  372.5 7.7 copy-start.23
  441.3 7.7 copy-start.12
  441.3 7.7 copy-start.23
  476.3 8.7 %slice-start.1 = ((s8[6291456]{0:T(1024)(128)(4,1)}), s8[4194304]{0:T(1024)(128)(4,1)S(1)}, s32[]{:S(2)}) async-start(s8[6291456]{0:T(1024)(128)(4,1)} %bitcast.224), calls=%async_computation.8 | async-start | bytes 8388608
  479.2 5.8 slice-start.2
  482.1 10.6 %slice-start.3 = ((s8[6291456]{0:T(1024)(128)(4,1)}), s8[4194304]{0:T(1024)(128)(4,1)S(1)}, s32[]{:S(2)}) async-start(s8[6291456]{0:T(1024)(128)(4,1)} %bitcast.226), calls=%async_computation.10 | async-start | bytes 8388608
  485.0 7.7 copy-start.29
  485.1 7.7 slice-start.4
  500.4 14.4 %copy-start.59 = (s32[288]{0:T(512)S(1)}, s32[288]{0:T(512)}, u32[]{:S(2)}) copy-start(s32[288]{0:T(512)} %copy-done.58) | copy-start | bytes 3460
  615.4 42.8 %copy-start.44 = (f32[12,768]{1,0:T(8,128)S(1)}, f32[12,768]{1,0:T(8,128)}, u32[]{:S(2)}) copy-start(f32[12,768]{1,0:T(8,128)} %param.22) | copy-start | bytes 110596
  615.4 42.7 %copy-start.51 = (f32[12,768]{1,0:T(8,128)S(1)}, f32[12,768]{1,0:T(8,128)}, u32[]{:S(2)}) copy-start(f32[12,768]{1,0:T(8,128)} %param.24) | copy-start | bytes 110596
  615.4 42.7 %copy-start.52 = (f32[12,768]{1,0:T(8,128)S(1)}, f32[12,768]{1,0:T(8,128)}, u32[]{:S(2)}) copy-start(f32[12,768]{1,0:T(8,128)} %param.23) | copy-start | bytes 110596
  665.1 192.1 %copy-start.22 = (f32[10,32,768]{2,1,0:T(8,128)S(1)}, f32[10,32,768]{2,1,0:T(8,128)}, u32[]{:S(2)}) copy-start(f32[10,32,768]{2,1,0:T(8,128)} %param.19) | copy-start | bytes 2949124
  665.1 192.1 %copy-start.36 = (f32[10,32,768]{2,1,0:T(8,128)S(1)}, f32[10,32,768]{2,1,0:T(8,128)}, u32[]{:S(2)}) copy-start(f32[10,32,768]{2,1,0:T(8,128)} %param.21) | copy-start | bytes 2949124
  665.1 192.1 %copy-start.37 = (f32[10,32,768]{2,1,0:T(8,128)S(1)}, f32[10,32,768]{2,1,0:T(8,128)}, u32[]{:S(2)}) copy-start(f32[10,32,768]{2,1,0:T(8,128)} %param.20) | copy-start | bytes 2949124
  (60 other events, 165.5 us)
Sparse Core Ops, SparseCore 0:
  11.5 112.7 all-gather.1
  576.7 280.4 reduce-scatter.1
where the time goes:
time: 878 us; the launch traced here: 867 us
  waiting for transfers between devices  296 us (34%)
  matrix products  262 us (30%)
  local copies, waits for them, and re-layouts  175 us (20%)
  blocking collectives  59.1 us (7%)
  other arithmetic  55 us (6%)
  between operations  16 us (2%)
    reduce_scatter x1, waiting for transfers between devices, local(): lax.psum_scatter(slot_grads, ('seq', 'batch'), scatter_dimension=0, tiled...  189 us
    all_gather x1, waiting for transfers between devices, local(): gathered = lax.all_gather(sending, ('seq', 'batch'), axis=0, tiled=True)  106 us
    dot_general x6, matrix products, contract_cols(): lax.dot_general(left, right, (((1,), (1,)), ((), ())), preferred_element_...  64.3 us
    scatter x1, local copies, waits for them, and re-layouts, local(): slot_grads = jnp.zeros((devices * capacity,) + weight_slots.shape[1:], jn...  61.8 us
    dot_general x2, matrix products, attend_back(): jnp.einsum('hqk,qhd->khd', d_scores, query_heads, preferred_element_type=...  45.4 us
    psum x1, blocking collectives, local(): small_grad = lax.psum(small_local, ('seq', 'batch'))  41.2 us
    dot_general x2, matrix products, attend_back(): jnp.einsum('hqk,khd->qhd', d_scores, key_heads, preferred_element_type=jn...  38.5 us
    dot_general x6, matrix products, contract_rows(): lax.dot_general(left, right, (((0,), (0,)), ((), ())), preferred_element_...  28.9 us
  transfers between devices with their start and end apart: 3, of which 3 were waited for; matrix products, arithmetic and copies ran while one was open for 5% of the time, Pallas kernels for 0%

commit v1 on v0

--- a/solution.py
+++ b/solution.py
@@ -3,6 +3,7 @@
 
 import jax
 import jax.numpy as jnp
+import numpy as np
 from jax import lax
 from jax.sharding import PartitionSpec as P
 
@@ -16,6 +17,127 @@
 adam_eps = 1e-08
 learn_rate = 0.2
 decay_rate = 0.01
+
+
+RING_ROUNDS = 5
+LINKS = ("x", "y", "u", "d")
+NEW_BLOCK = {
+    (0, 0, "x"): (1, 0, 0), (0, 0, "y"): (0, 1, 0), (0, 0, "d"): (0, 0, 1),
+    (0, 1, "x"): (1, 0, 1), (0, 1, "y"): (1, 1, 0), (0, 1, "d"): (0, 0, 2),
+    (0, 2, "x"): (1, 0, 2), (0, 2, "y"): (0, 1, 2), (0, 2, "d"): (0, 0, 3),
+    (0, 3, "x"): (1, 0, 3), (0, 3, "y"): (0, 1, 3), (0, 3, "d"): (1, 1, 2),
+    (0, 4, "x"): (1, 1, 3), (0, 4, "y"): (1, 1, 1), (0, 4, "d"): (0, 1, 1),
+    (1, 0, "x"): (1, 0, 1), (1, 0, "y"): (0, 1, 1), (1, 0, "u"): (0, 0, 0), (1, 0, "d"): (0, 0, 2),
+    (1, 1, "x"): (1, 0, 2), (1, 1, "y"): (0, 1, 2), (1, 1, "u"): (1, 0, 0), (1, 1, "d"): (0, 0, 3),
+    (1, 2, "x"): (1, 1, 2), (1, 2, "y"): (0, 1, 3), (1, 2, "u"): (0, 1, 0), (1, 2, "d"): (1, 0, 3),
+    (1, 3, "x"): (1, 1, 0), (1, 3, "y"): (1, 1, 3), (1, 3, "d"): (1, 1, 1),
+}
+DUMMY = 16
+
+
+def neighbour(chip, link):
+    if link == "x":
+        return chip ^ 1
+    if link == "y":
+        return chip ^ 2
+    if link == "u":
+        return chip - 4 if chip >= 4 else None
+    return chip + 4 if chip < 12 else None
+
+
+def received_block(chip, turn, link):
+    layer = chip >> 2
+    if layer < 2:
+        block = NEW_BLOCK.get((layer, turn, link))
+        if block is None:
+            return None
+        return block[2] * 4 + ((chip & 3) ^ (block[1] * 2 + block[0]))
+    block = NEW_BLOCK.get((3 - layer, turn, {"u": "d", "d": "u"}.get(link, link)))
+    if block is None:
+        return None
+    return (3 - block[2]) * 4 + ((chip & 3) ^ (block[1] * 2 + block[0]))
+
+
+def build_schedule():
+    rounds, columns = [], []
+    for turn in range(RING_ROUNDS):
+        moves = []
+        for link in LINKS:
+            pairs, takes, gives = [], [DUMMY] * 16, [DUMMY] * 16
+            for chip in range(16):
+                block = received_block(chip, turn, link)
+                if block is None:
+                    continue
+                source = neighbour(chip, link)
+                pairs.append((source, chip))
+                takes[chip] = block
+                gives[source] = block
+            if pairs:
+                moves.append((tuple(pairs), len(columns)))
+                columns.append(takes)
+                columns.append(gives)
+        rounds.append(moves)
+    return rounds, np.array(columns, np.int32).T
+
+
+ROUNDS, TABLE = build_schedule()
+SWAP = ((0, 1), (1, 0))
+
+
+def schedule_row():
+    return jnp.asarray(TABLE)[lax.axis_index("batch")]
+
+
+def take_block(blocks, index):
+    return lax.dynamic_index_in_dim(blocks, index, 0, keepdims=False)
+
+
+def put_block(blocks, block, index):
+    return lax.dynamic_update_index_in_dim(blocks, block, index, 0)
+
+
+def gather_blocks(own):
+    row = schedule_row()
+    me = lax.axis_index("batch")
+    both = jnp.zeros((2 * (DUMMY + 1),) + own.shape, own.dtype)
+    both = put_block(both, own, me)
+    both = put_block(both, lax.ppermute(own, "seq", SWAP), DUMMY + 1 + me)
+    for turn, moves in enumerate(ROUNDS):
+        arrived = []
+        for pairs, column in moves:
+            give = own if turn == 0 else take_block(both, row[column + 1])
+            arrived.append((lax.ppermute(give, "batch", pairs), row[column]))
+        for block, place in arrived:
+            both = put_block(both, block, place)
+            both = put_block(both, lax.ppermute(block, "seq", SWAP), DUMMY + 1 + place)
+    return both
+
+
+def reduce_blocks(blocks):
+    row = schedule_row()
+    me = lax.axis_index("batch")
+    for turn in reversed(range(RING_ROUNDS)):
+        arrived = []
+        for pairs, column in ROUNDS[turn]:
+            give = take_block(blocks, row[column])
+            back = tuple((target, source) for source, target in pairs)
+            arrived.append((lax.ppermute(give, "batch", back), row[column + 1]))
+        if turn > 0:
+            for block, place in arrived:
+                blocks = put_block(blocks, take_block(blocks, place) + block, place)
+    total = take_block(blocks, me).astype(jnp.float32)
+    for block, place in arrived:
+        total = total + block.astype(jnp.float32)
+    return total
+
+
+def sum_everywhere(values):
+    size = lax.axis_size("batch")
+    bit = 1
+    while bit < size:
+        values = values + lax.ppermute(values, "batch", [(i, i ^ bit) for i in range(size)])
+        bit *= 2
+    return values + lax.ppermute(values, "seq", SWAP)
 
 
 def slot_table(owners, capacity):
@@ -85,8 +207,16 @@
     hidden_width = (small_params.shape[0] - 8) * features
     slot_of = slot_table(owners, capacity)
     sending = weight_slots.astype(jnp.bfloat16)
-    gathered = lax.all_gather(sending, ("seq", "batch"), axis=0, tiled=True)
-    weight_stack = jnp.take(gathered, slot_of, axis=0).reshape(-1, features)
+    custom = lax.axis_size("batch") == 16 and lax.axis_size("seq") == 2
+    if custom:
+        gathered = gather_blocks(sending).reshape((-1,) + sending.shape[1:])
+        rank = slot_of - owners * capacity
+        other = (owners // 16) != lax.axis_index("seq")
+        place = (jnp.where(other, DUMMY + 1, 0) + owners % 16) * capacity + rank
+    else:
+        gathered = lax.all_gather(sending, ("seq", "batch"), axis=0, tiled=True)
+        place = slot_of
+    weight_stack = jnp.take(gathered, place, axis=0).reshape(-1, features)
     w_query = weight_stack[0:features]
     w_key = weight_stack[features : 2 * features]
     w_value = weight_stack[2 * features : 3 * features]
@@ -138,10 +268,7 @@
     attn_out = product(context_flat, w_out) + small_params[6]
     mixed_rows, norm_one_pull = jax.vjp(layer_norm, tokens_wide + attn_out, gain_one, shift_one)
     mixed_low = mixed_rows.astype(jnp.bfloat16).reshape(tokens.shape)
-    ffn_in, cot_in = (
-        lax.all_to_all(mixed_low, "seq", split_axis=0, concat_axis=1, tiled=True),
-        lax.all_to_all(grad_out, "seq", split_axis=0, concat_axis=1, tiled=True),
-    )
+    ffn_in, cot_in = mixed_low, grad_out
     ffn_rows = ffn_in.reshape(-1, features)
     cot_rows = cot_in.reshape(-1, features).astype(jnp.float32)
     hidden_pre = contract_cols(ffn_rows, w_hidden) + bias_hidden
@@ -156,10 +283,7 @@
     d_w_hidden = contract_rows(d_pre, ffn_rows)
     d_ffn_in = (d_residual + product(d_pre, w_hidden)).astype(jnp.bfloat16).reshape(ffn_in.shape)
     layer_low = layer_rows.astype(jnp.bfloat16).reshape(ffn_in.shape)
-    layer_out, d_mixed = (
-        lax.all_to_all(layer_low, "seq", split_axis=1, concat_axis=0, tiled=True),
-        lax.all_to_all(d_ffn_in, "seq", split_axis=1, concat_axis=0, tiled=True),
-    )
+    layer_out, d_mixed = layer_low, d_ffn_in
     d_summed, d_gain_one, d_shift_one = norm_one_pull(
         d_mixed.reshape(-1, features).astype(jnp.float32)
     )
@@ -228,12 +352,26 @@
     )
     panels = grad_stack.reshape(-1, weight_slots.shape[1], features)
     devices = lax.axis_size("seq") * lax.axis_size("batch")
-    slot_grads = (
-        jnp.zeros((devices * capacity,) + weight_slots.shape[1:], jnp.float32)
+    panel_at = (
+        jnp.full((devices * capacity,), panels.shape[0], jnp.int32)
         .at[slot_of]
-        .set(panels)
-    )
-    grad_slots = lax.psum_scatter(slot_grads, ("seq", "batch"), scatter_dimension=0, tiled=True)
+        .set(jnp.arange(panels.shape[0], dtype=jnp.int32))
+    )
+    padded = jnp.concatenate(
+        [panels.astype(jnp.bfloat16), jnp.zeros((1,) + panels.shape[1:], jnp.bfloat16)], axis=0
+    )
+    slot_grads = jnp.take(padded, panel_at, axis=0)
+    if custom:
+        by_core = slot_grads.reshape((2, 16, capacity) + panels.shape[1:])
+        core = lax.axis_index("seq")
+        kept = take_block(by_core, core)
+        blocks = kept + lax.ppermute(take_block(by_core, 1 - core), "seq", SWAP)
+        blocks = jnp.concatenate([blocks, jnp.zeros_like(blocks[:1])], axis=0)
+        grad_slots = reduce_blocks(blocks)
+    else:
+        grad_slots = lax.psum_scatter(
+            slot_grads, ("seq", "batch"), scatter_dimension=0, tiled=True
+        ).astype(jnp.float32)
     small_rows = jnp.stack(
         [
             d_gain_one,
@@ -247,7 +385,10 @@
         ]
     )
     small_local = jnp.concatenate([small_rows, column_sum(d_pre).reshape(-1, features)], axis=0)
-    small_grad = lax.psum(small_local, ("seq", "batch"))
+    if custom:
+        small_grad = sum_everywhere(small_local)
+    else:
+        small_grad = lax.psum(small_local, ("seq", "batch"))
     new_slots, new_first_slots, new_second_slots = adam_update(
         weight_slots, first_slots, second_slots, grad_slots, step_count
     )

time: 878 us -> 832 us (0.948)
  waiting for transfers between devices: 296 us -> 76.3 us
  between operations: 16 us -> 128 us
  starting transfers between devices: 3.76 us -> 88.7 us
  blocking collectives: 59.1 us -> 0 us
  other arithmetic: 55 us -> 77.8 us
  local copies, waits for them, and re-layouts: 175 us -> 185 us
    reduce_scatter x1 -> x0, waiting for transfers between devices: 189 us -> none  [local(): lax.psum_scatter(slot_grads, ('seq', 'batch'), scatter_dimension=0, tiled...]
    all_gather x1 -> x0, waiting for transfers between devices: 106 us -> none  [local(): gathered = lax.all_gather(sending, ('seq', 'batch'), axis=0, tiled=True)]
    ppermute x0 -> x67, starting transfers between devices: none -> 88.7 us  [the longest x20 39.5 us: reduce_blocks(): arrived.append((lax.ppermute(give, 'batch', back), row[column + 1]))]
    ppermute x0 -> x67, waiting for transfers between devices: none -> 76.3 us  [the longest x20 38.5 us: reduce_blocks(): arrived.append((lax.ppermute(give, 'batch', back), row[column + 1]))]
    scatter x1, local copies, waits for them, and re-layouts: 61.8 us -> 2.91 us  [local(): panel_at = jnp.full((devices * capacity,), panels.shape[0], jnp.int32).at...]
    psum x1 -> x0, blocking collectives: 41.2 us -> none  [local(): small_grad = lax.psum(small_local, ('seq', 'batch'))]
    dynamic_update_slice x0 -> x37, local copies, waits for them, and re-layouts: none -> 30.4 us  [put_block(): return lax.dynamic_update_index_in_dim(blocks, block, index, 0)]
    squeeze x0 -> x10, local copies, waits for them, and re-layouts: none -> 22.8 us  [take_block(): return lax.dynamic_index_in_dim(blocks, index, 0, keepdims=False)]
  transfers between devices with their start and end apart: 3 -> 67, of which waited for: 3 -> 19; matrix products, arithmetic and copies ran while one was open for 5% -> 11% of each run, Pallas kernels for 0% -> 0%
where the time goes in v1:
time: 832 us; the launch traced here: 821 us
  matrix products  264 us (32%)
  local copies, waits for them, and re-layouts  185 us (22%)
  between operations  128 us (15%)
  starting transfers between devices  88.7 us (11%)
  other arithmetic  77.8 us (9%)
  waiting for transfers between devices  76.3 us (9%)
    dot_general x6, matrix products, contract_cols(): lax.dot_general(left, right, (((1,), (1,)), ((), ())), preferred_element_...  71.1 us
    dot_general x2, matrix products, attend_back(): jnp.einsum('hqk,qhd->khd', d_scores, query_heads, preferred_element_type=...  45.4 us
    ppermute x20, starting transfers between devices, reduce_blocks(): arrived.append((lax.ppermute(give, 'batch', back), row[column + 1]))  39.5 us
    dot_general x2, matrix products, attend_back(): jnp.einsum('hqk,khd->qhd', d_scores, key_heads, preferred_element_type=jn...  39 us
    ppermute x20, waiting for transfers between devices, reduce_blocks(): arrived.append((lax.ppermute(give, 'batch', back), row[column + 1]))  38.5 us
    ppermute x20, starting transfers between devices, gather_blocks(): arrived.append((lax.ppermute(give, 'batch', pairs), row[column]))  35.6 us
    dynamic_update_slice x37, local copies, waits for them, and re-layouts, put_block(): return lax.dynamic_update_index_in_dim(blocks, block, index, 0)  30.4 us
    dot_general x6, matrix products, product(): return jnp.dot(left, right, preferred_element_type=jnp.float32)  28.7 us
  transfers between devices with their start and end apart: 67, of which 19 were waited for; matrix products, arithmetic and copies ran while one was open for 11% of the time, Pallas kernels for 0%

profile of v1, /device:TPU:0, one launch (start us, length us, event | category | flops | bytes accessed | tf_op | source)
XLA Modules:
  0.0 821.3 jit_solution(6056021349705698273)
XLA Ops:
  0.7 6.0 broadcast_in_dim.291
  213.7 18.0 %gather_fusion = bf16[288,32,768]{2,1,0:T(8,128)(2,1)} fusion(bf16[340,32,768]{2,1,0:T(8,128)(2,1)} %bitcast.112, s32[1024]{0:T(1024)S(1)} %pad_clamp_fusion.1), kind=kCustom, calls=%fused_computation | custom fusion | bytes 28312704 | tf_op jit(solution)/shard_map/jit(_take)/gather | solution.py:219
  231.7 7.8 broadcast_select_fusion.1
  246.4 8.7 %fusion.130 = (bf16[96,32,768]{2,1,0:T(8,128)(2,1)}, bf16[96,32,768]{2,1,0:T(8,128)(2,1)}) fusion(bf16[288,32,768]{2,1,0:T(8,128)(2,1)} %copy-done.3), kind=kLoop, calls=%fused_computation.336 | loop fusion | bytes 18874368 | tf_op jit(solution)/shard_map/slice | solution.py:225
  277.5 23.9 %while.26 = (s32[]{:T(128)}, bf16[2,512,768]{2,1,0:T(8,128)(2,1)}, f32[2,12,512]{2,1,0:T(8,128)}, bf16[2,512,12,64]{1,3,2,0:T(8,128)(2,1)}, pred[2,512]{1,0:T(4,...) while((s32[]{:T(128)}, bf16[2,512,768]{2,1,0:T(8,128)(2,1)}, ...), condition=%wide.region_4.5_spmd, body=%wide.region_1.4_spmd.sunk | while | flops 843442176 | bytes 50557560 | solution.py:264
  306.5 37.3 %multiply_convert_fusion.2 = (bf16[1024,3072]{1,0:T(8,128)(2,1)S(1)}, f32[1024,3072]{1,0:T(8,128)}, f32[1024,3072]{1,0:T(8,128)}) fusion(f32[3072]{0:T(1024)S(1)} %copy-done.60, bf16[3072,768]{1,0:T(8,128)(2,1)} %bitcast.496, f32[1024,768]{1,0:T(8,128)S(1)} %get-tuple-element.319, f32[768]{0:T(1024)S(1)} %copy-done.62, f32[768]{0:T(1024)S(1)} %copy-done.50, ...), kind=kOutput, calls=%fused_computation.83 | convolution fusion | flops 5043388416 | bytes 39348224 | tf_op jit(solution)/shard_map/dot_general | solution.py:181
  356.3 18.8 %convert_reduce_fusion = (f32[3072]{0:T(1024)}, bf16[1024,3072]{1,0:T(8,128)(2,1)}) fusion(f32[1024,3072]{1,0:T(8,128)} %get-tuple-element.222, bf16[1024,768]{1,0:T(8,128)(2,1)} %get-tuple-element.210, bf16[3072,768]{1,0:T(8,128)(2,1)} %bitcast.498, f32[1024,3072]{1,0:T(8,128)} %get-tuple-element.320, f32[3072]{0:T(1024)S(1)} %copy-done.60), kind=kOutput, calls=%fused_computation.81 | convolution fusion | flops 4885312512 | bytes 37773312 | tf_op jit(solution)/shard_map/dot_general | solution.py:181
  375.1 10.0 %fusion.93 = (f32[768]{0:T(1024)}, f32[1024]{0:T(1024)S(1)}, f32[768]{0:T(1024)}, bf16[1024,768]{1,0:T(8,128)(2,1)S(1)}) fusion(f32[1024,768]{1,0:T(8,128)S(1)} %get-tuple-element.319, f32[1024]{0:T(1024)S(1)} %fusion.114, f32[1024]{0:T(1024)S(1)} %broadcast_multiply_fusion.1, f32[768]{0:T(1024)S(1)} %copy-done.50, ...), kind=kOutput, calls=%fused_computation.111 | convolution fusion | flops 4841272320 | bytes 18899968 | tf_op jit(solution)/shard_map/dot_general | solution.py:171
  390.2 138.7 %while.27 = (s32[]{:T(128)}, bf16[2,512,768]{1,2,0:T(8,128)(2,1)}, bf16[2,512,768]{1,2,0:T(8,128)(2,1)}, bf16[2,512,768]{1,2,0:T(8,128)(2,1)}, bf16[2,512,12,64]...) while((s32[]{:T(128)}, bf16[2,512,768]{1,2,0:T(8,128)(2,1)}, ...), condition=%wide.region_15.16_spmd, body=%wide.region_13.15_spmd.sunk | while | flops 2097034240 | bytes 185809680 | solution.py:322
  391.8 7.7 fusion.205
  399.5 6.4 fusion.206
  406.7 22.7 %multiply_convert_fusion.6 = bf16[12,64,512]{2,1,0:T(8,128)(2,1)S(1)} fusion(f32[12,512,512]{1,2,0:T(8,128)} %fusion.205, f32[12,512,512]{1,2,0:T(8,128)} %fusion.206, f32[12,512]{1,0:T(8,128)S(1)} %dynamic-slice_bitcast_fusion.39, pred[512]{0:T(512)(128)(4,1)S(1)} %dynamic-slice_reduce_fusion.5, ...), kind=kOutput, calls=%fused_computation.44.clone.1 | convolution fusion | flops 438049280 | bytes 51971584 | tf_op jit(solution)/shard_map/while/body/eval_jaxpr/hqk,qhd->khd/dot_general | solution.py:311
  429.5 7.7 fusion.207
  439.0 19.6 %multiply_convert_fusion.5 = bf16[12,64,512]{2,1,0:T(8,128)(2,1)S(1)} fusion(f32[12,512,512]{1,2,0:T(8,128)} %fusion.205, f32[12,512,512]{1,2,0:T(8,128)} %fusion.206, f32[12,512]{1,0:T(8,128)S(1)} %dynamic-slice_bitcast_fusion.39, pred[512]{0:T(512)(128)(4,1)S(1)} %dynamic-slice_reduce_fusion.5, bf16[2,512,12,64]{1,3,2,0:T(8,128)(2,1)} %get-tuple-element.490, ...), kind=kOutput, calls=%fused_computation.45.clone.1 | convolution fusion | flops 438049280 | bytes 51971584 | tf_op jit(solution)/shard_map/while/body/eval_jaxpr/hqk,khd->qhd/dot_general | solution.py:307
  460.9 7.7 fusion.205
  468.6 6.4 fusion.206
  475.8 22.7 %multiply_convert_fusion.6 = bf16[12,64,512]{2,1,0:T(8,128)(2,1)S(1)} fusion(f32[12,512,512]{1,2,0:T(8,128)} %fusion.205, f32[12,512,512]{1,2,0:T(8,128)} %fusion.206, f32[12,512]{1,0:T(8,128)S(1)} %dynamic-slice_bitcast_fusion.39, pred[512]{0:T(512)(128)(4,1)S(1)} %dynamic-slice_reduce_fusion.5, ...), kind=kOutput, calls=%fused_computation.44.clone.1 | convolution fusion | flops 438049280 | bytes 51971584 | tf_op jit(solution)/shard_map/while/body/eval_jaxpr/hqk,qhd->khd/dot_general | solution.py:311
  498.6 7.7 fusion.207
  508.1 19.4 %multiply_convert_fusion.5 = bf16[12,64,512]{2,1,0:T(8,128)(2,1)S(1)} fusion(f32[12,512,512]{1,2,0:T(8,128)} %fusion.205, f32[12,512,512]{1,2,0:T(8,128)} %fusion.206, f32[12,512]{1,0:T(8,128)S(1)} %dynamic-slice_bitcast_fusion.39, pred[512]{0:T(512)(128)(4,1)S(1)} %dynamic-slice_reduce_fusion.5, bf16[2,512,12,64]{1,3,2,0:T(8,128)(2,1)} %get-tuple-element.490, ...), kind=kOutput, calls=%fused_computation.45.clone.1 | convolution fusion | flops 438049280 | bytes 51971584 | tf_op jit(solution)/shard_map/while/body/eval_jaxpr/hqk,khd->qhd/dot_general | solution.py:307
  539.6 6.3 fusion.89
  546.0 5.6 fusion.88
  551.6 6.1 concatenate.14
  557.8 17.7 %gather_fusion.1 = bf16[320,32,768]{2,1,0:T(8,128)(2,1)} fusion(bf16[289,32,768]{2,1,0:T(8,128)(2,1)} %concatenate.14, s32[1024]{0:T(1024)S(1)} %copy-done.61), kind=kCustom, calls=%fused_computation.1 | custom fusion | bytes 31458560 | tf_op jit(solution)/shard_map/jit(_take)/gather | solution.py:363
  575.4 13.5 %broadcast_select_fusion = bf16[2,16,10,32,768]{4,3,2,1,0:T(8,128)(2,1)} fusion(bf16[2,16,10,32,768]{4,3,2,1,0:T(8,128)(2,1)} %bitcast.486, pred[2,16,10]{2,1,0:T(8,128)(4,1)S(1)} %copy-done.57), kind=kLoop, calls=%fused_computation.78 | loop fusion | flops 7864320 | bytes 31457600 | tf_op jit(solution)/shard_map/jit(_take)/select_n | solution.py:363
  589.0 7.3 dynamic-slice_bitcast_fusion.1
  598.1 10.9 %collective-permute-done.41 = bf16[16,10,32,768]{3,2,1,0:T(8,128)(2,1)} collective-permute-done((bf16[16,10,32,768]{3,2,1,0:T(8,128)(2,1)}, bf16[16,10,32,768]{3,2,1,0:T(8,128)(2,1)}, u32[]{:S(2)}, u32[]{:S(2)}) %collective-permute-start.41) | collective-permute-done | bytes 7864352 | tf_op jit(solution)/shard_map/ppermute | solution.py:368
  609.0 9.3 %bitcast_add_fusion = bf16[16,10,32,768]{3,2,1,0:T(8,128)(2,1)} fusion(bf16[16,10,32,768]{3,2,1,0:T(8,128)(2,1)} %collective-permute-done.41, bf16[2,16,10,32,768]{4,3,2,1,0:T(8,128)(2,1)} %broadcast_select_fusion, s32[]{:T(128)S(6)} %select_n.430), kind=kLoop, calls=%fused_computation.97 | loop fusion | flops 3932160 | bytes 23592964 | tf_op jit(solution)/shard_map/add | solution.py:368
  624.1 7.6 concatenate.15
  661.9 8.9 %collective-permute-done.46 = bf16[10,32,768]{2,1,0:T(8,128)(2,1)S(1)} collective-permute-done((bf16[10,32,768]{2,1,0:T(8,128)(2,1)S(1)}, bf16[10,32,768]{2,1,0:T(8,128)(2,1)S(1)}, u32[]{:S(2)}, u32[]{:S(2)}) %collective-permute-start.46) | collective-permute-done | bytes 491552 | tf_op jit(solution)/shard_map/ppermute | solution.py:124
  700.7 7.3 collective-permute-done.50
  718.9 7.2 collective-permute-start.53
  739.1 6.8 collective-permute-done.62
  (487 shorter events, 343.0 us)
Async XLA Ops:
  7.5 25.1 %collective-permute-start.1 = (bf16[10,32,768]{2,1,0:T(8,128)(2,1)S(1)}, bf16[10,32,768]{2,1,0:T(8,128)(2,1)S(1)}, u32[]{:S(2)}, u32[]{:S(2)}) collective-permute-start(bf16[10,32,768]{2,1,0:T(8,128)(2,1)S(1)} %get-tuple-element.226), channel_id=1, source_target_pairs={{1,0},{0,1},{3,2},{2,3},{5,4},{4,5},{7,6},{6,7},{9,8},{8,9},{11,10... | collective-permute-start | bytes 1474568 | tf_op jit(solution)/shard_map/ppermute | solution.py:109
  10.5 22.7 %collective-permute-start.3 = (bf16[10,32,768]{2,1,0:T(8,128)(2,1)S(1)}, bf16[10,32,768]{2,1,0:T(8,128)(2,1)S(1)}, u32[]{:S(2)}, u32[]{:S(2)}) collective-permute-start(bf16[10,32,768]{2,1,0:T(8,128)(2,1)S(1)} %get-tuple-element.226), channel_id=1, source_target_pairs={{2,0},{3,1},{0,2},{1,3},{6,4},{7,5},{4,6},{5,7},{10,8},{11,9},{8,1... | collective-permute-start | bytes 1474568 | tf_op jit(solution)/shard_map/ppermute | solution.py:109
  12.0 21.3 %collective-permute-start.5 = (bf16[10,32,768]{2,1,0:T(8,128)(2,1)S(1)}, bf16[10,32,768]{2,1,0:T(8,128)(2,1)S(1)}, u32[]{:S(2)}, u32[]{:S(2)}) collective-permute-start(bf16[10,32,768]{2,1,0:T(8,128)(2,1)S(1)} %get-tuple-element.226), channel_id=1, source_target_pairs={{0,4},{1,5},{2,6},{3,7},{4,8},{5,9},{6,10},{7,11},{8,12},{9,13},{1... | collective-permute-start | bytes 1474568 | tf_op jit(solution)/shard_map/ppermute | solution.py:109
  15.5 18.2 %collective-permute-start.7 = (bf16[10,32,768]{2,1,0:T(8,128)(2,1)S(1)}, bf16[10,32,768]{2,1,0:T(8,128)(2,1)S(1)}, u32[]{:S(2)}, u32[]{:S(2)}) collective-permute-start(bf16[10,32,768]{2,1,0:T(8,128)(2,1)S(1)} %get-tuple-element.226), channel_id=1, source_target_pairs={{4,0},{5,1},{6,2},{7,3},{8,4},{9,5},{10,6},{11,7},{12,8},{13,9},{1... | collective-permute-start | bytes 1474568 | tf_op jit(solution)/shard_map/ppermute | solution.py:109
  16.8 17.0 %collective-permute-start = (bf16[10,32,768]{2,1,0:T(8,128)(2,1)S(1)}, bf16[10,32,768]{2,1,0:T(8,128)(2,1)S(1)}, u32[]{:S(2)}, u32[]{:S(2)}) collective-permute-start(bf16[10,32,768]{2,1,0:T(8,128)(2,1)S(1)} %get-tuple-element.226), channel_id=1, source_target_pairs={{0,16},{16,0},{1,17},{17,1},{2,18},{18,2},{3,19},{19,3},{4,20},{20... | collective-permute-start | bytes 1474568 | tf_op jit(solution)/shard_map/ppermute | solution.py:104
  58.3 19.3 %collective-permute-start.11 = (bf16[10,32,768]{2,1,0:T(8,128)(2,1)}, bf16[10,32,768]{2,1,0:T(8,128)(2,1)S(1)}, u32[]{:S(2)}, u32[]{:S(2)}) collective-permute-start(bf16[10,32,768]{2,1,0:T(8,128)(2,1)} %get-tuple-element.245), channel_id=1, source_target_pairs={{2,0},{3,1},{0,2},{1,3},{6,4},{7,5},{4,6},{5,7},{10,8},{11,9},{8,1... | collective-permute-start | bytes 1474568 | tf_op jit(solution)/shard_map/ppermute | solution.py:109
  58.8 19.4 %collective-permute-start.13 = (bf16[10,32,768]{2,1,0:T(8,128)(2,1)S(1)}, bf16[10,32,768]{2,1,0:T(8,128)(2,1)S(1)}, u32[]{:S(2)}, u32[]{:S(2)}) collective-permute-start(bf16[10,32,768]{2,1,0:T(8,128)(2,1)S(1)} %get-tuple-element.244), channel_id=1, source_target_pairs={{0,4},{1,5},{2,6},{3,7},{4,8},{5,9},{6,10},{7,11},{8,12},{9,13},{1... | collective-permute-start | bytes 1474568 | tf_op jit(solution)/shard_map/ppermute | solution.py:109
  63.4 14.8 %collective-permute-start.15 = (bf16[10,32,768]{2,1,0:T(8,128)(2,1)S(1)}, bf16[10,32,768]{2,1,0:T(8,128)(2,1)S(1)}, u32[]{:S(2)}, u32[]{:S(2)}) collective-permute-start(bf16[10,32,768]{2,1,0:T(8,128)(2,1)S(1)} %get-tuple-element.243), channel_id=1, source_target_pairs={{4,0},{5,1},{6,2},{7,3},{8,4},{9,5},{10,6},{11,7},{12,8},{13,9},{1... | collective-permute-start | bytes 1474568 | tf_op jit(solution)/shard_map/ppermute | solution.py:109
  64.7 13.9 %collective-permute-start.10 = (bf16[10,32,768]{2,1,0:T(8,128)(2,1)S(1)}, bf16[10,32,768]{2,1,0:T(8,128)(2,1)S(1)}, u32[]{:S(2)}, u32[]{:S(2)}) collective-permute-start(bf16[10,32,768]{2,1,0:T(8,128)(2,1)S(1)} %collective-permute-done.9), channel_id=1, source_target_pairs={{0,16},{16,0},{1,17},{17,1},{2,18},{18,2},{3,19},{19,3},{4,20},{20... | collective-permute-start | bytes 1474568 | tf_op jit(solution)/shard_map/ppermute | solution.py:112
  101.1 19.6 %collective-permute-start.19 = (bf16[10,32,768]{2,1,0:T(8,128)(2,1)}, bf16[10,32,768]{2,1,0:T(8,128)(2,1)S(1)}, u32[]{:S(2)}, u32[]{:S(2)}) collective-permute-start(bf16[10,32,768]{2,1,0:T(8,128)(2,1)} %get-tuple-element.241), channel_id=1, source_target_pairs={{2,0},{3,1},{0,2},{1,3},{6,4},{7,5},{4,6},{5,7},{10,8},{11,9},{8,1... | collective-permute-start | bytes 1474568 | tf_op jit(solution)/shard_map/ppermute | solution.py:109
  102.7 18.6 %collective-permute-start.21 = (bf16[10,32,768]{2,1,0:T(8,128)(2,1)S(1)}, bf16[10,32,768]{2,1,0:T(8,128)(2,1)S(1)}, u32[]{:S(2)}, u32[]{:S(2)}) collective-permute-start(bf16[10,32,768]{2,1,0:T(8,128)(2,1)S(1)} %get-tuple-element.240), channel_id=1, source_target_pairs={{0,4},{1,5},{2,6},{3,7},{4,8},{5,9},{6,10},{7,11},{8,12},{9,13},{1... | collective-permute-start | bytes 1474568 | tf_op jit(solution)/shard_map/ppermute | solution.py:109
  107.3 14.1 %collective-permute-start.23 = (bf16[10,32,768]{2,1,0:T(8,128)(2,1)S(1)}, bf16[10,32,768]{2,1,0:T(8,128)(2,1)S(1)}, u32[]{:S(2)}, u32[]{:S(2)}) collective-permute-start(bf16[10,32,768]{2,1,0:T(8,128)(2,1)S(1)} %get-tuple-element.239), channel_id=1, source_target_pairs={{4,0},{5,1},{6,2},{7,3},{8,4},{9,5},{10,6},{11,7},{12,8},{13,9},{1... | collective-permute-start | bytes 1474568 | tf_op jit(solution)/shard_map/ppermute | solution.py:109
  144.4 15.7 %collective-permute-start.27 = (bf16[10,32,768]{2,1,0:T(8,128)(2,1)}, bf16[10,32,768]{2,1,0:T(8,128)(2,1)S(1)}, u32[]{:S(2)}, u32[]{:S(2)}) collective-permute-start(bf16[10,32,768]{2,1,0:T(8,128)(2,1)} %get-tuple-element.237), channel_id=1, source_target_pairs={{2,0},{3,1},{0,2},{1,3},{6,4},{7,5},{4,6},{5,7},{10,8},{11,9},{8,1... | collective-permute-start | bytes 1474568 | tf_op jit(solution)/shard_map/ppermute | solution.py:109
  145.0 15.6 %collective-permute-start.29 = (bf16[10,32,768]{2,1,0:T(8,128)(2,1)S(1)}, bf16[10,32,768]{2,1,0:T(8,128)(2,1)S(1)}, u32[]{:S(2)}, u32[]{:S(2)}) collective-permute-start(bf16[10,32,768]{2,1,0:T(8,128)(2,1)S(1)} %get-tuple-element.236), channel_id=1, source_target_pairs={{4,8},{5,9},{6,10},{7,11},{8,12},{9,13},{10,14},{11,15},{20,24},{2... | collective-permute-start | bytes 1474568 | tf_op jit(solution)/shard_map/ppermute | solution.py:109
  145.7 17.2 %collective-permute-start.31 = (bf16[10,32,768]{2,1,0:T(8,128)(2,1)S(1)}, bf16[10,32,768]{2,1,0:T(8,128)(2,1)S(1)}, u32[]{:S(2)}, u32[]{:S(2)}) collective-permute-start(bf16[10,32,768]{2,1,0:T(8,128)(2,1)S(1)} %get-tuple-element.235), channel_id=1, source_target_pairs={{4,0},{5,1},{6,2},{7,3},{8,4},{9,5},{10,6},{11,7},{20,16},{21,17},... | collective-permute-start | bytes 1474568 | tf_op jit(solution)/shard_map/ppermute | solution.py:109
  147.0 15.9 %collective-permute-start.26 = (bf16[10,32,768]{2,1,0:T(8,128)(2,1)S(1)}, bf16[10,32,768]{2,1,0:T(8,128)(2,1)S(1)}, u32[]{:S(2)}, u32[]{:S(2)}) collective-permute-start(bf16[10,32,768]{2,1,0:T(8,128)(2,1)S(1)} %collective-permute-done.25), channel_id=1, source_target_pairs={{0,16},{16,0},{1,17},{17,1},{2,18},{18,2},{3,19},{19,3},{4,20},{20... | collective-permute-start | bytes 1474568 | tf_op jit(solution)/shard_map/ppermute | solution.py:112
  169.8 15.5 %collective-permute-start.33 = (bf16[10,32,768]{2,1,0:T(8,128)(2,1)S(1)}, bf16[10,32,768]{2,1,0:T(8,128)(2,1)S(1)}, u32[]{:S(2)}, u32[]{:S(2)}) collective-permute-start(bf16[10,32,768]{2,1,0:T(8,128)(2,1)S(1)} %dynamic-slice_bitcast_fusion.25), channel_id=1, source_target_pairs={{1,0},{0,1},{3,2},{2,3},{13,12},{12,13},{15,14},{14,15},{17,16},{1... | collective-permute-start | bytes 1474568 | tf_op jit(solution)/shard_map/ppermute | solution.py:109
  187.8 19.2 %collective-permute-start.35 = (bf16[10,32,768]{2,1,0:T(8,128)(2,1)}, bf16[10,32,768]{2,1,0:T(8,128)(2,1)S(1)}, u32[]{:S(2)}, u32[]{:S(2)}) collective-permute-start(bf16[10,32,768]{2,1,0:T(8,128)(2,1)} %get-tuple-element.233), channel_id=1, source_target_pairs={{2,0},{3,1},{0,2},{1,3},{14,12},{15,13},{12,14},{13,15},{18,16},{1... | collective-permute-start | bytes 1474568 | tf_op jit(solution)/shard_map/ppermute | solution.py:109
  191.1 16.3 %collective-permute-start.37 = (bf16[10,32,768]{2,1,0:T(8,128)(2,1)S(1)}, bf16[10,32,768]{2,1,0:T(8,128)(2,1)S(1)}, u32[]{:S(2)}, u32[]{:S(2)}) collective-permute-start(bf16[10,32,768]{2,1,0:T(8,128)(2,1)S(1)} %get-tuple-element.232), channel_id=1, source_target_pairs={{8,12},{9,13},{10,14},{11,15},{24,28},{25,29},{26,30},{27,31}} | collective-permute-start | bytes 1474568 | tf_op jit(solution)/shard_map/ppermute | solution.py:109
  191.8 15.7 %collective-permute-start.39 = (bf16[10,32,768]{2,1,0:T(8,128)(2,1)S(1)}, bf16[10,32,768]{2,1,0:T(8,128)(2,1)S(1)}, u32[]{:S(2)}, u32[]{:S(2)}) collective-permute-start(bf16[10,32,768]{2,1,0:T(8,128)(2,1)S(1)} %get-tuple-element.231), channel_id=1, source_target_pairs={{4,0},{5,1},{6,2},{7,3},{20,16},{21,17},{22,18},{23,19}} | collective-permute-start | bytes 1474568 | tf_op jit(solution)/shard_map/ppermute | solution.py:109
  193.3 14.6 %collective-permute-start.34 = (bf16[10,32,768]{2,1,0:T(8,128)(2,1)S(1)}, bf16[10,32,768]{2,1,0:T(8,128)(2,1)S(1)}, u32[]{:S(2)}, u32[]{:S(2)}) collective-permute-start(bf16[10,32,768]{2,1,0:T(8,128)(2,1)S(1)} %collective-permute-done.33), channel_id=1, source_target_pairs={{0,16},{16,0},{1,17},{17,1},{2,18},{18,2},{3,19},{19,3},{4,20},{20... | collective-permute-start | bytes 1474568 | tf_op jit(solution)/shard_map/ppermute | solution.py:112
  619.7 15.2 %collective-permute-start.42 = (bf16[10,32,768]{2,1,0:T(8,128)(2,1)S(1)}, bf16[10,32,768]{2,1,0:T(8,128)(2,1)S(1)}, u32[]{:S(2)}, u32[]{:S(2)}) collective-permute-start(bf16[10,32,768]{2,1,0:T(8,128)(2,1)S(1)} %get-tuple-element.280), channel_id=1, source_target_pairs={{0,1},{1,0},{2,3},{3,2},{12,13},{13,12},{14,15},{15,14},{16,17},{1... | collective-permute-start | bytes 1474568 | tf_op jit(solution)/shard_map/ppermute | solution.py:124
  637.2 14.3 %collective-permute-start.43 = (bf16[10,32,768]{2,1,0:T(8,128)(2,1)S(1)}, bf16[10,32,768]{2,1,0:T(8,128)(2,1)S(1)}, u32[]{:S(2)}, u32[]{:S(2)}) collective-permute-start(bf16[10,32,768]{2,1,0:T(8,128)(2,1)S(1)} %get-tuple-element.277), channel_id=1, source_target_pairs={{0,2},{1,3},{2,0},{3,1},{12,14},{13,15},{14,12},{15,13},{16,18},{1... | collective-permute-start | bytes 1474568 | tf_op jit(solution)/shard_map/ppermute | solution.py:124
  674.2 14.1 %collective-permute-start.47 = (bf16[10,32,768]{2,1,0:T(8,128)(2,1)S(1)}, bf16[10,32,768]{2,1,0:T(8,128)(2,1)S(1)}, u32[]{:S(2)}, u32[]{:S(2)}) collective-permute-start(bf16[10,32,768]{2,1,0:T(8,128)(2,1)S(1)} %get-tuple-element.271), channel_id=1, source_target_pairs={{0,2},{1,3},{2,0},{3,1},{4,6},{5,7},{6,4},{7,5},{8,10},{9,11},{10,... | collective-permute-start | bytes 1474568 | tf_op jit(solution)/shard_map/ppermute | solution.py:124
  711.0 16.1 %collective-permute-start.51 = (bf16[10,32,768]{2,1,0:T(8,128)(2,1)}, bf16[10,32,768]{2,1,0:T(8,128)(2,1)}, u32[]{:S(2)}, u32[]{:S(2)}) collective-permute-start(bf16[10,32,768]{2,1,0:T(8,128)(2,1)} %get-tuple-element.265), channel_id=1, source_target_pairs={{0,2},{1,3},{2,0},{3,1},{4,6},{5,7},{6,4},{7,5},{8,10},{9,11},{10,... | collective-permute-start | bytes 1474568 | tf_op jit(solution)/shard_map/ppermute | solution.py:124
  718.9 14.2 %collective-permute-start.53 = (bf16[10,32,768]{2,1,0:T(8,128)(2,1)}, bf16[10,32,768]{2,1,0:T(8,128)(2,1)S(1)}, u32[]{:S(2)}, u32[]{:S(2)}) collective-permute-start(bf16[10,32,768]{2,1,0:T(8,128)(2,1)} %get-tuple-element.263), channel_id=1, source_target_pairs={{0,4},{1,5},{2,6},{3,7},{4,8},{5,9},{6,10},{7,11},{8,12},{9,13},{1... | collective-permute-start | bytes 1474568 | tf_op jit(solution)/shard_map/ppermute | solution.py:124
  736.3 33.2 %collective-permute-start.54 = (bf16[10,32,768]{2,1,0:T(8,128)(2,1)}, bf16[10,32,768]{2,1,0:T(8,128)(2,1)}, u32[]{:S(2)}, u32[]{:S(2)}) collective-permute-start(bf16[10,32,768]{2,1,0:T(8,128)(2,1)} %get-tuple-element.262), channel_id=1, source_target_pairs={{0,1},{1,0},{2,3},{3,2},{4,5},{5,4},{6,7},{7,6},{8,9},{9,8},{10,11... | collective-permute-start | bytes 1474568 | tf_op jit(solution)/shard_map/ppermute | solution.py:124
  772.2 15.4 %collective-permute-start.55 = (bf16[10,32,768]{2,1,0:T(8,128)(2,1)}, bf16[10,32,768]{2,1,0:T(8,128)(2,1)}, u32[]{:S(2)}, u32[]{:S(2)}) collective-permute-start(bf16[10,32,768]{2,1,0:T(8,128)(2,1)} %get-tuple-element.259), channel_id=1, source_target_pairs={{0,2},{1,3},{2,0},{3,1},{4,6},{5,7},{6,4},{7,5},{8,10},{9,11},{10,... | collective-permute-start | bytes 1474568 | tf_op jit(solution)/shard_map/ppermute | solution.py:124
  780.3 31.4 %collective-permute-start.66 = (f32[12,768]{1,0:T(8,128)S(1)}, f32[12,768]{1,0:T(8,128)S(1)}, u32[]{:S(2)}, u32[]{:S(2)}) collective-permute-start(f32[12,768]{1,0:T(8,128)S(1)} %add.839), channel_id=1, source_target_pairs={{0,16},{16,0},{1,17},{17,1},{2,18},{18,2},{3,19},{19,3},{4,20},{20... | collective-permute-start | bytes 110600 | tf_op jit(solution)/shard_map/ppermute | solution.py:140
  780.4 15.7 %collective-permute-start.56 = (bf16[10,32,768]{2,1,0:T(8,128)(2,1)}, bf16[10,32,768]{2,1,0:T(8,128)(2,1)S(1)}, u32[]{:S(2)}, u32[]{:S(2)}) collective-permute-start(bf16[10,32,768]{2,1,0:T(8,128)(2,1)} %get-tuple-element.258), channel_id=1, source_target_pairs={{4,0},{5,1},{6,2},{7,3},{8,4},{9,5},{10,6},{11,7},{12,8},{13,9},{1... | collective-permute-start | bytes 1474568 | tf_op jit(solution)/shard_map/ppermute | solution.py:124
  781.9 16.2 %collective-permute-start.57 = (bf16[10,32,768]{2,1,0:T(8,128)(2,1)}, bf16[10,32,768]{2,1,0:T(8,128)(2,1)S(1)}, u32[]{:S(2)}, u32[]{:S(2)}) collective-permute-start(bf16[10,32,768]{2,1,0:T(8,128)(2,1)} %get-tuple-element.257), channel_id=1, source_target_pairs={{0,4},{1,5},{2,6},{3,7},{4,8},{5,9},{6,10},{7,11},{8,12},{9,13},{1... | collective-permute-start | bytes 1474568 | tf_op jit(solution)/shard_map/ppermute | solution.py:124
  802.6 13.8 %collective-permute-start.60 = (bf16[10,32,768]{2,1,0:T(8,128)(2,1)S(1)}, bf16[10,32,768]{2,1,0:T(8,128)(2,1)S(1)}, u32[]{:S(2)}, u32[]{:S(2)}) collective-permute-start(bf16[10,32,768]{2,1,0:T(8,128)(2,1)S(1)} %get-tuple-element.255), channel_id=1, source_target_pairs={{4,0},{5,1},{6,2},{7,3},{8,4},{9,5},{10,6},{11,7},{12,8},{13,9},{1... | collective-permute-start | bytes 1474568 | tf_op jit(solution)/shard_map/ppermute | solution.py:124
  (121 other events, 1844.1 us)

commit v2 on v0

v2 whole, which is shorter than its diff:
```python
from functools import partial
import math

import jax
import jax.numpy as jnp
import numpy as np
from jax import lax
from jax.experimental import pallas as pl
from jax.experimental.pallas import tpu as pltpu
from jax.sharding import PartitionSpec as P

beta_first = 0.9
beta_second = 0.999
adam_eps = 1e-08
learn_rate = 0.2
decay_rate = 0.01
SWAP = ((0, 1), (1, 0))

HEAD_DIM = 64
PANEL = 32
norm_eps = 1e-06
masked_score = -30.0
LANES = 128
BF = jnp.bfloat16
F32 = jnp.float32


def mm(a, b):
    return lax.dot_general(a, b, (((1,), (0,)), ((), ())), preferred_element_type=F32)


def mm_nt(a, b):
    return lax.dot_general(a, b, (((1,), (1,)), ((), ())), preferred_element_type=F32)


def mm_tn(a, b):
    return lax.dot_general(a, b, (((0,), (0,)), ((), ())), preferred_element_type=F32)


def normalize(z):
    centre = z - jnp.mean(z, axis=-1, keepdims=True)
    rstd = lax.rsqrt(jnp.mean(centre * centre, axis=-1, keepdims=True) + norm_eps)
    return centre * rstd, rstd


def norm_back(zh, rstd, t):
    mean_t = jnp.mean(t, axis=-1, keepdims=True)
    mean_tz = jnp.mean(t * zh, axis=-1, keepdims=True)
    return (t - mean_t - zh * mean_tz) * rstd


def lane_half(shape, half):
    lane = lax.broadcasted_iota(jnp.int32, shape, len(shape) - 1)
    return (lane < HEAD_DIM) if half == 0 else (lane >= HEAD_DIM)


def rows_of(panels, start, count):
    return panels[start // PANEL:(start + count) // PANEL].reshape(count, panels.shape[-1])


def fetch_panels(slots, first, target, place, sem):
    def one(i, carry):
        pltpu.make_async_copy(slots.at[place[first + i]], target.at[i], sem).start()
        return carry
    lax.fori_loop(0, target.shape[0], one, 0)


def fetch_wait(slots, target, sem):
    pltpu.make_async_copy(slots.at[pl.ds(0, target.shape[0])], target, sem).wait()


def send_panels(stage, first, slots, place, sem):
    def one(i, carry):
        pltpu.make_async_copy(stage.at[i], slots.at[place[first + i]], sem).start()
        return carry
    lax.fori_loop(0, stage.shape[0], one, 0)


def send_wait(stage, slots, sem):
    pltpu.make_async_copy(stage, slots.at[pl.ds(0, stage.shape[0])], sem).wait()


def attn_fwd_kernel(limits, place, x_ref, slots_ref, small_ref, q_ref, k_ref, v_ref, c_ref, p_ref,
                    mixed_ref, zh_ref, rstd_ref, w_ref, w_sem):
    step = pl.program_id(0)
    pairs = x_ref.shape[-1] // LANES
    seq, pair = step // pairs, step % pairs
    d = x_ref.shape[-1]
    block = x_ref.shape[1]

    @pl.when(step == 0)
    def _():
        fetch_panels(slots_ref, 0, w_ref, place, w_sem)
        fetch_wait(slots_ref, w_ref, w_sem)

    @pl.when(pair == 0)
    def _():
        x = x_ref[0]
        q = mm(x, rows_of(w_ref, 0, d)) + small_ref[4:5, :]
        q_ref[0] = (q.astype(BF).astype(F32) * 0.125).astype(BF)
        k_ref[0] = mm(x, rows_of(w_ref, d, d)).astype(BF)
        v_ref[0] = (mm(x, rows_of(w_ref, 2 * d, d)) + small_ref[5:6, :]).astype(BF)

    lanes = pl.ds(pl.multiple_of(pair * LANES, LANES), LANES)
    qp, kp, vp = q_ref[0, :, lanes], k_ref[0, :, lanes], v_ref[0, :, lanes]
    vt = vp.T
    limit = limits[seq]
    key = lax.broadcasted_iota(jnp.int32, (block, block), 0)
    parts = []
    for half in range(2):
        km = jnp.where(lane_half(kp.shape, half), kp, jnp.zeros_like(kp))
        s = mm_nt(km, qp)
        s = jnp.where(key < limit, s, masked_score)
        top = jnp.max(s, axis=0, keepdims=True)
        e = jnp.exp(s - top)
        total = jnp.sum(e, axis=0, keepdims=True)
        p = (e * (1.0 / total)).astype(BF)
        p_ref[half] = p
        parts.append(mm(vt[half * HEAD_DIM:(half + 1) * HEAD_DIM], p))
    ctx_t = jnp.concatenate(parts, axis=0)
    c_ref[0, :, lanes] = ctx_t.T.astype(BF)

    @pl.when(pair == pairs - 1)
    def _():
        u = x_ref[0].astype(F32) + mm(c_ref[0], rows_of(w_ref, 3 * d, d)) + small_ref[6:7, :]
        zh, rstd = normalize(u)
        zh_ref[0] = zh
        rstd_ref[0] = rstd
        mixed_ref[0] = (zh * small_ref[0:1, :] + small_ref[1:2, :]).astype(BF)


def attn_fwd(x, gathered, small, limits, place):
    seqs, block, d = x.shape
    pairs = d // LANES
    by_seq = lambda shape: pl.BlockSpec((1,) + shape, lambda i, lim, pr: (i // pairs, 0, 0))
    whole = lambda a: pl.BlockSpec(a, lambda i, lim, pr: (0, 0), pipeline_mode=pl.Buffered(1))
    act = jax.ShapeDtypeStruct((seqs, block, d), BF)
    return pl.pallas_call(
        attn_fwd_kernel,
        grid_spec=pltpu.PrefetchScalarGridSpec(
            num_scalar_prefetch=2,
            grid=(seqs * pairs,),
            in_specs=[by_seq((block, d)), pl.BlockSpec(memory_space=pl.ANY), whole(small.shape)],
            out_specs=[by_seq((block, d))] * 4
            + [pl.BlockSpec((2, block, block), lambda i, lim, pr: (i, 0, 0))]
            + [by_seq((block, d)), by_seq((block, d)), by_seq((block, 1))],
            scratch_shapes=[pltpu.VMEM((4 * d // PANEL, PANEL, d), BF), pltpu.SemaphoreType.DMA],
        ),
        out_shape=[act, act, act, act,
                   jax.ShapeDtypeStruct((seqs * 2 * pairs, block, block), BF),
                   act,
                   jax.ShapeDtypeStruct((seqs, block, d), F32),
                   jax.ShapeDtypeStruct((seqs, block, 1), F32)],
        compiler_params=pltpu.CompilerParams(vmem_limit_bytes=56 << 20, dimension_semantics=("arbitrary",)),
        name="attn_fwd",
    )(limits, place, x, gathered, small)


ROWS = 256
CHUNK = 512


def ffn_kernel(place, back, mixed_ref, go_ref, w_hbm, small_ref, bh_ref,
               out_ref, dmixed_ref, sums_ref, dbh_ref, slots_ref,
               w1, w2, hid, gp, acc, df, dyb, stage, w_sem, s_sem):
    d = mixed_ref.shape[-1]
    tokens = mixed_ref.shape[0]
    ff = bh_ref.shape[1]
    chunks = ff // CHUNK
    tiles = tokens // ROWS
    panels = CHUNK // PANEL
    first1 = 4 * d // PANEL
    first2 = first1 + ff // PANEL

    def start(c, carry):
        fetch_panels(w_hbm, first1 + c * panels, w1.at[c], place, w_sem.at[0, c])
        fetch_panels(w_hbm, first2 + c * panels, w2.at[c], place, w_sem.at[1, c])
        return carry

    lax.fori_loop(0, chunks, start, 0)

    def up(c, carry):
        fetch_wait(w_hbm, w1.at[c], w_sem.at[0, c])
        fetch_wait(w_hbm, w2.at[c], w_sem.at[1, c])
        cols = pl.ds(pl.multiple_of(c * CHUNK, CHUNK), CHUNK)
        w1c, w2c = w1[c].reshape(CHUNK, d), w2[c].reshape(CHUNK, d)
        bias = bh_ref[0:1, cols]
        for r in range(tiles):
            rows = pl.ds(r * ROWS, ROWS)
            f = mm_nt(mixed_ref[rows, :], w1c) + bias
            half_erf = 0.5 * lax.erf(f * (1.0 / math.sqrt(2.0))) + 0.5
            h = (f * half_erf).astype(BF)
            hid[rows, cols] = h
            gp[rows, cols] = (half_erf + f * (jnp.exp(-0.5 * f * f) * (1.0 / math.sqrt(2.0 * math.pi)))).astype(BF)
            part = mm(h, w2c)
            acc[rows, :] = jnp.where(c == 0, part, acc[rows, :] + part)
        return carry

    lax.fori_loop(0, chunks, up, 0)

    sums_ref[...] = jnp.zeros_like(sums_ref)

    def middle(r, carry):
        rows = pl.ds(pl.multiple_of(r * ROWS, ROWS), ROWS)
        rr = mixed_ref[rows, :].astype(F32) + acc[rows, :] + small_ref[7:8, :]
        zh, rstd = normalize(rr)
        out_ref[rows, :] = (zh * small_ref[2:3, :] + small_ref[3:4, :]).astype(BF)
        e = go_ref[rows, :].astype(F32)
        dr = norm_back(zh, rstd, e * small_ref[2:3, :])
        dy = dr.astype(BF)
        dyb[rows, :] = dy
        acc[rows, :] = dr
        sums_ref[0:1, :] += jnp.sum(e * zh, axis=0, keepdims=True)
        sums_ref[1:2, :] += jnp.sum(e, axis=0, keepdims=True)
        sums_ref[2:3, :] += jnp.sum(dy.astype(F32), axis=0, keepdims=True)
        return carry

    lax.fori_loop(0, tiles, middle, 0)

    def down(c, carry):
        cols = pl.ds(pl.multiple_of(c * CHUNK, CHUNK), CHUNK)
        w1c, w2c = w1[c].reshape(CHUNK, d), w2[c].reshape(CHUNK, d)
        dbh = jnp.zeros((1, CHUNK), F32)
        for r in range(tiles):
            rows = pl.ds(r * ROWS, ROWS)
            dfr = (mm_nt(dyb[rows, :], w2c) * gp[rows, cols].astype(F32)).astype(BF)
            df[rows, :] = dfr
            dbh += jnp.sum(dfr.astype(F32), axis=0, keepdims=True)
            acc[rows, :] += mm(dfr, w1c)
        dbh_ref[0:1, cols] = dbh

        @pl.when(c > 0)
        def _():
            send_wait(stage.at[0], slots_ref, s_sem.at[0])
            send_wait(stage.at[1], slots_ref, s_sem.at[1])

        stage[0] = mm_tn(df[...], mixed_ref[...]).astype(BF).reshape(panels, PANEL, d)
        send_panels(stage.at[0], first1 + c * panels, slots_ref, back, s_sem.at[0])
        stage[1] = mm_tn(hid[:, cols], dyb[...]).astype(BF).reshape(panels, PANEL, d)
        send_panels(stage.at[1], first2 + c * panels, slots_ref, back, s_sem.at[1])
        return carry

    lax.fori_loop(0, chunks, down, 0)
    dmixed_ref[...] = acc[...].astype(BF)
    send_wait(stage.at[0], slots_ref, s_sem.at[0])
    send_wait(stage.at[1], slots_ref, s_sem.at[1])


def ffn(mixed, go, gathered, small, bh, place, back, slots):
    tokens, d = mixed.shape
    ff = bh.shape[1]
    full = lambda shape: pl.BlockSpec(shape, lambda i, pr, bk: (0,) * len(shape))
    return pl.pallas_call(
        ffn_kernel,
        grid_spec=pltpu.PrefetchScalarGridSpec(
            num_scalar_prefetch=2,
            grid=(1,),
            in_specs=[full((tokens, d)), full((tokens, d)), pl.BlockSpec(memory_space=pl.ANY),
                      full(small.shape), full(bh.shape)],
            out_specs=[full((tokens, d)), full((tokens, d)), full((8, d)), full((1, ff)),
                       pl.BlockSpec(memory_space=pl.ANY)],
            scratch_shapes=[
                pltpu.VMEM((ff // CHUNK, CHUNK // PANEL, PANEL, d), BF),
                pltpu.VMEM((ff // CHUNK, CHUNK // PANEL, PANEL, d), BF),
                pltpu.VMEM((tokens, ff), BF), pltpu.VMEM((tokens, ff), BF),
                pltpu.VMEM((tokens, d), F32), pltpu.VMEM((tokens, CHUNK), BF),
                pltpu.VMEM((tokens, d), BF), pltpu.VMEM((2, CHUNK // PANEL, PANEL, d), BF),
                pltpu.SemaphoreType.DMA((2, ff // CHUNK)), pltpu.SemaphoreType.DMA((2,)),
            ],
        ),
        out_shape=[jax.ShapeDtypeStruct((tokens, d), BF), jax.ShapeDtypeStruct((tokens, d), BF),
                   jax.ShapeDtypeStruct((8, d), F32), jax.ShapeDtypeStruct((1, ff), F32),
                   jax.ShapeDtypeStruct((slots, PANEL, d), BF)],
        compiler_params=pltpu.CompilerParams(vmem_limit_bytes=60 << 20, dimension_semantics=("arbitrary",)),
        name="ffn",
    )(place, back, mixed, go, gathered, small, bh)


def attn_bwd_kernel(limits, place, back, dmixed_ref, zh_ref, rstd_ref, x_ref, q_ref, k_ref, v_ref,
                    c_ref, p_ref, w_hbm, small_ref, slots_in,
                    gin_ref, sums_ref, slots_ref,
                    dctx, dq, dk, dv, dw, stage, w_ref, s_sem, w_sem):
    step = pl.program_id(0)
    pairs = x_ref.shape[-1] // LANES
    seq, pair = step // pairs, step % pairs
    d = x_ref.shape[-1]
    block = x_ref.shape[1]
    tiles = block // ROWS

    @pl.when(step == 0)
    def _():
        fetch_panels(w_hbm, 0, w_ref, place, w_sem)
        dw[...] = jnp.zeros_like(dw)
        sums_ref[...] = jnp.zeros_like(sums_ref)
        fetch_wait(w_hbm, w_ref, w_sem)

    @pl.when(pair == 0)
    def _():
        for r in range(tiles):
            rows = pl.ds(r * ROWS, ROWS)
            e = dmixed_ref[0, rows, :].astype(F32)
            zh = zh_ref[0, rows, :]
            du = norm_back(zh, rstd_ref[0, rows, :], e * small_ref[0:1, :])
            da = du.astype(BF)
            gin_ref[0, rows, :] = du
            sums_ref[0:1, :] += jnp.sum(e * zh, axis=0, keepdims=True)
            sums_ref[1:2, :] += jnp.sum(e, axis=0, keepdims=True)
            sums_ref[4:5, :] += jnp.sum(da.astype(F32), axis=0, keepdims=True)
            dctx[rows, :] = mm_nt(da, rows_of(w_ref, 3 * d, d)).astype(BF)
            dw[pl.ds(3 * d, d), :] += mm_tn(c_ref[0, rows, :], da)

    lanes = pl.ds(pl.multiple_of(pair * LANES, LANES), LANES)
    qp, kp, vp, dcp = q_ref[0, :, lanes], k_ref[0, :, lanes], v_ref[0, :, lanes], dctx[:, lanes]
    kt = kp.T
    limit = limits[seq]
    key = lax.broadcasted_iota(jnp.int32, (block, block), 0)
    prod_t = (dcp.astype(F32) * c_ref[0, :, lanes].astype(F32)).T
    dqt, dks, dvs = [], [], []
    for half in range(2):
        vm = jnp.where(lane_half(vp.shape, half), vp, jnp.zeros_like(vp))
        dp = mm_nt(vm, dcp)
        delta = jnp.sum(prod_t[half * HEAD_DIM:(half + 1) * HEAD_DIM], axis=0, keepdims=True)
        p = p_ref[half]
        ds = jnp.where(key < limit, p.astype(F32) * (dp - delta), 0.0).astype(BF)
        dqt.append(mm(kt[half * HEAD_DIM:(half + 1) * HEAD_DIM], ds))
        dks.append(mm(ds, qp))
        dvs.append(mm(p, dcp))
    low = lane_half(qp.shape, 0)
    dq[:, lanes] = (jnp.concatenate(dqt, axis=0) * 0.125).T.astype(BF)
    dk[:, lanes] = jnp.where(low, dks[0], dks[1]).astype(BF)
    dv[:, lanes] = jnp.where(low, dvs[0], dvs[1]).astype(BF)

    @pl.when(pair == pairs - 1)
    def _():
        x = x_ref[0]
        gin_ref[0] += (mm_nt(dq[...], rows_of(w_ref, 0, d)) + mm_nt(dk[...], rows_of(w_ref, d, d))
                       + mm_nt(dv[...], rows_of(w_ref, 2 * d, d)))
        dw[pl.ds(0, d), :] += mm_tn(x, dq[...])
        dw[pl.ds(d, d), :] += mm_tn(x, dk[...])
        dw[pl.ds(2 * d, d), :] += mm_tn(x, dv[...])
        sums_ref[2:3, :] += jnp.sum(dq[...].astype(F32), axis=0, keepdims=True)
        sums_ref[3:4, :] += jnp.sum(dv[...].astype(F32), axis=0, keepdims=True)

    @pl.when(step == pl.num_programs(0) - 1)
    def _():
        stage[...] = dw[...].astype(BF).reshape(stage.shape)
        send_panels(stage, 0, slots_ref, back, s_sem)
        send_wait(stage, slots_ref, s_sem)


def attn_bwd(dmixed, zh, rstd, x, q, k, v, c, p, gathered, small, limits, place, back, slots):
    seqs, block, d = x.shape
    pairs = d // LANES
    by_seq = lambda shape: pl.BlockSpec((1,) + shape, lambda i, lim, pr, bk: (i // pairs, 0, 0))
    whole = lambda a: pl.BlockSpec(a, lambda i, lim, pr, bk: (0, 0), pipeline_mode=pl.Buffered(1))
    return pl.pallas_call(
        attn_bwd_kernel,
        grid_spec=pltpu.PrefetchScalarGridSpec(
            num_scalar_prefetch=3,
            grid=(seqs * pairs,),
            in_specs=[by_seq((block, d)), by_seq((block, d)), by_seq((block, 1))]
            + [by_seq((block, d))] * 5
            + [pl.BlockSpec((2, block, block), lambda i, lim, pr, bk: (i, 0, 0)),
               pl.BlockSpec(memory_space=pl.ANY), whole(small.shape), pl.BlockSpec(memory_space=pl.ANY)],
            out_specs=[by_seq((block, d)), pl.BlockSpec((8, d), lambda i, lim, pr, bk: (0, 0)),
                       pl.BlockSpec(memory_space=pl.ANY)],
            scratch_shapes=[pltpu.VMEM((block, d), BF)] * 4
            + [pltpu.VMEM((4 * d, d), F32), pltpu.VMEM((4 * d // PANEL, PANEL, d), BF),
               pltpu.VMEM((4 * d // PANEL, PANEL, d), BF), pltpu.SemaphoreType.DMA, pltpu.SemaphoreType.DMA],
        ),
        out_shape=[jax.ShapeDtypeStruct((seqs, block, d), F32), jax.ShapeDtypeStruct((8, d), F32),
                   jax.ShapeDtypeStruct(slots.shape, BF)],
        input_output_aliases={14: 2},
        compiler_params=pltpu.CompilerParams(vmem_limit_bytes=60 << 20, dimension_semantics=("arbitrary",)),
        name="attn_bwd",
    )(limits, place, back, dmixed, zh, rstd, x, q, k, v, c, p, gathered, small, slots)


def slot_table(owners, capacity):
    panel_index = jnp.arange(owners.shape[0], dtype=jnp.int32)
    same_owner = (owners[:, None] == owners[None, :]) & (
        panel_index[None, :] < panel_index[:, None]
    )
    rank_within = jnp.sum(same_owner.astype(jnp.int32), axis=1)
    return owners * capacity + rank_within


def adam_update(weight, first_old, second_old, grad_now, step_count):
    step_float = step_count[0].astype(jnp.float32)
    first_new = beta_first * first_old + (1.0 - beta_first) * grad_now
    second_new = beta_second * second_old + (1.0 - beta_second) * grad_now * grad_now
    first_hat = first_new / (1.0 - jnp.power(beta_first, step_float))
    second_hat = second_new / (1.0 - jnp.power(beta_second, step_float))
    weight_new = weight - learn_rate * (
        first_hat / (jnp.sqrt(second_hat) + adam_eps) + decay_rate * weight
    )
    return (weight_new, first_new, second_new)


def sum_everywhere(values):
    size = lax.axis_size("batch")
    bit = 1
    while bit < size:
        values = values + lax.ppermute(values, "batch", [(i, i ^ bit) for i in range(size)])
        bit *= 2
    return values + lax.ppermute(values, "seq", SWAP)


def local(
    tokens,
    grad_out,
    lengths,
    owners,
    weight_slots,
    first_slots,
    second_slots,
    small_params,
    small_first,
    small_second,
    step_count,
):
    capacity = weight_slots.shape[0]
    block_rows, features = tokens.shape[1:]
    slot_of = slot_table(owners, capacity)
    devices = lax.axis_size("seq") * lax.axis_size("batch")
    device = lax.axis_index("seq") * lax.axis_size("batch") + lax.axis_index("batch")
    limits = lengths - lax.axis_index("seq") * block_rows
    gathered = lax.all_gather(weight_slots.astype(BF), ("seq", "batch"), axis=0, tiled=True)
    q, k, v, ctx, probs, mixed, zh, rstd = attn_fwd(tokens, gathered, small_params, limits, slot_of)
    bias_hidden = small_params[8:].reshape(1, -1)
    layer_out, d_mixed, sums_ffn, d_bias, slots = ffn(
        mixed.reshape(-1, features), grad_out.reshape(-1, features), gathered, small_params,
        bias_hidden, slot_of, slot_of, devices * capacity)
    grad_in, sums_attn, slots = attn_bwd(
        d_mixed.reshape(tokens.shape), zh, rstd, tokens, q, k, v, ctx, probs, gathered,
        small_params, limits, slot_of, slot_of, slots)
    grad_slots = lax.psum_scatter(
        slots, ("seq", "batch"), scatter_dimension=0, tiled=True).astype(jnp.float32)
    held = jnp.sum((owners == device).astype(jnp.int32))
    used = jnp.arange(capacity, dtype=jnp.int32) < held
    grad_slots = jnp.where(used[:, None, None], grad_slots, 0.0)
    small_local = jnp.concatenate(
        [sums_attn[0:2], sums_ffn[0:2], sums_attn[2:5], sums_ffn[2:3],
         d_bias.reshape(-1, features)], axis=0)
    small_grad = sum_everywhere(small_local)
    new_slots, new_first_slots, new_second_slots = adam_update(
        weight_slots, first_slots, second_slots, grad_slots, step_count
    )
    new_small, new_small_first, new_small_second = adam_update(
        small_params, small_first, small_second, small_grad, step_count
    )
    return (
        layer_out.reshape(tokens.shape),
        grad_in,
        grad_slots,
        new_slots,
        new_first_slots,
        new_second_slots,
        small_grad,
        new_small,
        new_small_first,
        new_small_second,
    )


def solution(mesh):
    in_specs = (
        P("batch", "seq", None),
        P("batch", "seq", None),
        P("batch"),
        P(),
        P(("seq", "batch"), None, None),
        P(("seq", "batch"), None, None),
        P(("seq", "batch"), None, None),
        P(),
        P(),
        P(),
        P(),
    )
    out_specs = (
        P("batch", "seq", None),
        P("batch", "seq", None),
        P(("seq", "batch"), None, None),
        P(("seq", "batch"), None, None),
        P(("seq", "batch"), None, None),
        P(("seq", "batch"), None, None),
        P(),
        P(),
        P(),
        P(),
    )
    return jax.shard_map(local, mesh=mesh, in_specs=in_specs, out_specs=out_specs, check_vma=False)
```

time: 878 us -> 429 us (0.49); the launches traced: 867 us -> 429 us
  matrix products: 262 us -> 0 us
  local copies, waits for them, and re-layouts: 175 us -> 4.33 us
  Pallas kernels: 0 us -> 125 us
  blocking collectives: 59.1 us -> 0 us
  other arithmetic: 55 us -> 9.38 us
  waiting for transfers between devices: 296 us -> 269 us
    dot_general x32 -> x0, matrix products: 262 us -> none  [the longest x6 64.3 us: contract_cols(): lax.dot_general(left, right, (((1,), (1,)), ((), ())), preferred_element_...]
    pallas_call x0 -> x3, Pallas kernels: none -> 125 us  [the longest x1 54 us: ffn(): pl.pallas_call(ffn_kernel, grid_spec=pltpu.PrefetchScalarGridSpec(num_sca...]
    scatter x1 -> x0, local copies, waits for them, and re-layouts: 61.8 us -> none  [local(): slot_grads = jnp.zeros((devices * capacity,) + weight_slots.shape[1:], jn...]
    reduce_scatter x1, waiting for transfers between devices: 189 us -> 145 us  [local(): lax.psum_scatter(slots, ('seq', 'batch'), scatter_dimension=0, tiled=True)]
    psum x1 -> x0, blocking collectives: 41.2 us -> none  [local(): small_grad = lax.psum(small_local, ('seq', 'batch'))]
    unnamed x4 -> x0, other arithmetic: 22.7 us -> none
    unnamed x162 -> x22, local copies, waits for them, and re-layouts: 24.5 us -> 2.03 us
    reshape x11 -> x1, local copies, waits for them, and re-layouts: 22.1 us -> 0.01 us  [local(): d_bias.reshape(-1, features)]
  transfers between devices with their start and end apart: 3 -> 7, of which waited for: 3 -> 6; matrix products, arithmetic and copies ran while one was open for 5% -> 2% of each run, Pallas kernels for 0% -> 0%
where the time goes in v2:
time: 429 us
  waiting for transfers between devices  269 us (63%)
  Pallas kernels  125 us (29%)
  between operations  15 us (3%)
  other arithmetic  9.38 us (2%)
  starting transfers between devices  5.6 us (1%)
  local copies, waits for them, and re-layouts  4.33 us (1%)
    reduce_scatter x1, waiting for transfers between devices, local(): lax.psum_scatter(slots, ('seq', 'batch'), scatter_dimension=0, tiled=True)  145 us
    all_gather x1, waiting for transfers between devices, local(): lax.all_gather(weight_slots.astype(BF), ('seq', 'batch'), axis=0, tiled=T...  112 us
    pallas_call x1, Pallas kernels, ffn(): pl.pallas_call(ffn_kernel, grid_spec=pltpu.PrefetchScalarGridSpec(num_sca...  54 us
    pallas_call x1, Pallas kernels, attn_bwd(): pl.pallas_call(attn_bwd_kernel, grid_spec=pltpu.PrefetchScalarGridSpec(nu...  39.7 us
    pallas_call x1, Pallas kernels, attn_fwd(): pl.pallas_call(attn_fwd_kernel, grid_spec=pltpu.PrefetchScalarGridSpec(nu...  31.4 us
    ppermute x4, waiting for transfers between devices, sum_everywhere(): lax.ppermute(values, 'batch', [(i, i ^ bit) for i in range(size)])  12.5 us
  transfers between devices with their start and end apart: 7, of which 6 were waited for; matrix products, arithmetic and copies ran while one was open for 2% of the time, Pallas kernels for 0%

profile of v2, /device:TPU:0, one launch (start us, length us, event | category | flops | bytes accessed | tf_op | source)
XLA Modules:
  0.0 428.6 jit_solution(9134616437124795399)
XLA Ops:
  7.2 0.0 all-gather.2.cloned.1.call-start
  7.2 2.0 convert_element_type.18
  9.3 0.0 all-gather.2.cloned.1.call-update
  9.3 0.0 reduce-scatter.2.cloned.1.call-start
  9.4 0.7 slice_bitcast_fusion
  10.1 0.6 copy.22
  10.7 0.2 convert_reduce_fusion
  10.9 0.5 broadcast_subtract_fusion.limits
  11.5 1.2 convert_reduce_fusion.1
  12.7 111.6 %all-gather.2.cloned.1.call-done.slots_ref.w_hbm = bf16[320,32,768]{2,1,0:T(8,128)(2,1)} async-done(((bf16[10,32,768]{2,1,0:T(8,128)(2,1)}), bf16[320,32,768]{2,1,0:T(8,128)(2,1)}) %all-gather.2.cloned.1.call-update) | async-done | bytes 15728656 | tf_op jit(solution)/shard_map/all_gather | solution.py:428
  124.3 31.4 %attn_fwd.1 = (bf16[2,512,768]{2,1,0:T(8,128)(2,1)}, bf16[2,512,768]{2,1,0:T(8,128)(2,1)}, bf16[2,512,768]{2,1,0:T(8,128)(2,1)}, bf16[2,512,768]{2,1,0:T(8,128)(...) custom-call(s32[2]{0:T(128)} %broadcast_subtract_fusion.limits, ...), custom_call_target="tpu_custom_call" | custom-call | tf_op jit(solution)/shard_map/attn_fwd/pallas_call | solution.py:138
  155.7 54.0 %ffn.1 = (bf16[1024,768]{1,0:T(8,128)(2,1)}, bf16[1024,768]{1,0:T(8,128)(2,1)}, f32[8,768]{1,0:T(8,128)}, f32[1,3072]{1,0:T(1,128)}, bf16[320,32,768]{2,1,0:T(8,128)(2,1)}) custom-call(s32[288]{0:T(512)} %get-tuple-element.51.place.back, s32[288]{0:T(512)} %get-tuple-element.51.place.back, bf16[1024,768]{1,0:T(8,128)(2,1)} %bitcast.12, ...), custom_call_target="tpu_custom_call" | custom-call | tf_op jit(solution)/shard_map/ffn/pallas_call | solution.py:253
  209.7 39.7 %attn_bwd.1 = (f32[2,512,768]{2,1,0:T(8,128)}, f32[8,768]{1,0:T(8,128)}, bf16[320,32,768]{2,1,0:T(8,128)(2,1)}) custom-call(s32[2]{0:T(128)} %broadcast_subtract_fusion.limits, s32[288]{0:T(512)} %get-tuple-element.51.place.back, s32[288]{0:T(512)} %get-tuple-element.51.place.back, bf16[2,512,768]{2,1,0:T(8,128)(2,1)} %bitcast.10, ...), custom_call_target="tpu_custom_call", output_to_operand_aliasing={{2}: (14, {})} | custom-call | tf_op jit(solution)/shard_map/attn_bwd/pallas_call | solution.py:356
  249.5 0.0 reduce-scatter.2.cloned.1.call-update
  249.6 0.6 copy-done.7
  250.2 1.0 slice.17
  251.2 0.7 slice.19
  251.9 0.5 broadcast.9
  252.4 0.7 reduce.3
  253.2 1.5 collective-permute-start
  254.6 2.7 collective-permute-done
  257.3 1.5 collective-permute-start.1
  258.9 2.6 collective-permute-done.1
  261.5 0.5 collective-permute-start.2
  262.0 3.6 collective-permute-done.2
  265.7 2.0 collective-permute-start.3
  267.6 3.5 collective-permute-done.3
  271.1 0.1 collective-permute-start.4
  271.2 0.7 iota_compare_fusion.1
  272.7 0.7 multiply_subtract_fusion.1
  273.3 145.1 %reduce-scatter.2.cloned.1.call-done = bf16[10,32,768]{2,1,0:T(8,128)(2,1)} async-done(((bf16[320,32,768]{2,1,0:T(8,128)(2,1)}), bf16[10,32,768]{2,1,0:T(8,128)(2,1)}) %reduce-scatter.2.cloned.1.call-update) | async-done | bytes 491536 | tf_op jit(solution)/shard_map/reduce_scatter | solution.py:437
  418.4 3.3 multiply_subtract_fusion
  (28 shorter events, 0.2 us)
Async XLA Ops:
  7.2 3.5 copy-start.6
  7.2 3.8 copy-start.9
  7.2 117.1 %all-gather.2.cloned.1.call-start = ((), (), s32[]{:S(2)}) async-start(), calls=%async_computation.1 | async-start | bytes 16220160 | tf_op jit(solution)/shard_map/all_gather | solution.py:428
  9.3 409.1 %reduce-scatter.2.cloned.1.call-start = ((), (), s32[]{:S(2)}) async-start(), calls=%async_computation.2 | async-start | bytes 16220160 | tf_op jit(solution)/shard_map/reduce_scatter | solution.py:437
  249.4 0.7 copy-start.7
  249.5 3.0 copy-start.8
  249.5 23.2 %copy-start.3 = (f32[12,768]{1,0:T(8,128)S(1)}, f32[12,768]{1,0:T(8,128)}, u32[]{:S(2)}) copy-start(f32[12,768]{1,0:T(8,128)} %small_ref.5) | copy-start | bytes 110596
  249.5 23.2 %copy-start.4 = (f32[12,768]{1,0:T(8,128)S(1)}, f32[12,768]{1,0:T(8,128)}, u32[]{:S(2)}) copy-start(f32[12,768]{1,0:T(8,128)} %param.20) | copy-start | bytes 110596
  249.5 23.2 %copy-start.5 = (f32[12,768]{1,0:T(8,128)S(1)}, f32[12,768]{1,0:T(8,128)}, u32[]{:S(2)}) copy-start(f32[12,768]{1,0:T(8,128)} %param.19) | copy-start | bytes 110596
  249.5 168.9 %copy-start.1 = (f32[10,32,768]{2,1,0:T(8,128)S(1)}, f32[10,32,768]{2,1,0:T(8,128)}, u32[]{:S(2)}) copy-start(f32[10,32,768]{2,1,0:T(8,128)} %param.17) | copy-start | bytes 2949124
  249.5 168.9 %copy-start.2 = (f32[10,32,768]{2,1,0:T(8,128)S(1)}, f32[10,32,768]{2,1,0:T(8,128)}, u32[]{:S(2)}) copy-start(f32[10,32,768]{2,1,0:T(8,128)} %param.16) | copy-start | bytes 2949124
  249.5 168.9 %copy-start = (f32[10,32,768]{2,1,0:T(8,128)S(1)}, f32[10,32,768]{2,1,0:T(8,128)}, u32[]{:S(2)}) copy-start(f32[10,32,768]{2,1,0:T(8,128)} %param.15) | copy-start | bytes 2949124
  253.2 4.1 collective-permute-start
  257.3 4.1 collective-permute-start.1
  261.5 4.1 collective-permute-start.2
  265.7 5.5 %collective-permute-start.3 = (f32[12,768]{1,0:T(8,128)S(1)}, f32[12,768]{1,0:T(8,128)S(1)}, u32[]{:S(2)}, u32[]{:S(2)}) collective-permute-start(f32[12,768]{1,0:T(8,128)S(1)} %add.62), channel_id=1, source_target_pairs={{0,8},{1,9},{2,10},{3,11},{4,12},{5,13},{6,14},{7,15},{8,0},{9,1},... | collective-permute-start | bytes 110600 | tf_op jit(solution)/shard_map/ppermute | solution.py:404
  271.1 1.5 collective-permute-start.4
Sparse Core Ops, SparseCore 0:
  11.5 112.7 all-gather.1
  249.7 168.6 reduce-scatter.1
